TPU v7x, 256 devices: a whole 4x4x8 slice. The times are simulated.
256 devices in a mesh: row: 32 (over z, x), layer: 8 (over y, core).
Axes of the slice: x: 4, y: 4, z: 8, core: 2. Of those that a mesh axis runs over, the one named last changes fastest.
Arguments:
- window_points: int32 [2, 32768], P(None, 'row'), may hold values from 0 to 63
- pivot_points: int32 [2, 512], replicated, may hold values from 0 to 63
- window_factor: bfloat16 [32768, 16384], P('row', 'layer'), may hold values from -1.5 to 1.5
- pivot_factor: bfloat16 [512, 16384], P('row', 'layer'), may hold values from -0.0234375 to 0.0234375
- right_sides: bfloat16 [32768, 512], P('row', 'layer'), may hold values from -6 to 6
- pivot_sides: bfloat16 [512, 512], P('row', 'layer'), may hold values from -6 to 6
Outputs:
- panel_factor: float32 [32768, 512], P('row', 'layer')
- eliminated: float32 [32768, 512], P('row', 'layer')
All inputs are finite; a program needn't handle non-finite values.
Results may differ from a plain program's by a relative error of at most 0.0006.
Values may be sent and summed in bfloat16 or wider, within the bound.
No kernel may reach another device: no remote copies, remote signals or barrier semaphores. Data moves between devices by JAX's collectives and lax.ppermute only.
A program may use at most 64 MiB of HBM per device.

v0:
```python
import jax
import jax.numpy as jnp
from jax import lax
from jax.experimental import pallas as pl
from jax.experimental.pallas import tpu as pltpu
from jax.sharding import PartitionSpec as P


nugget_value = 2.0
variance_value = 4.0
length_scale = 4.0


F32 = jnp.float32
BF16 = jnp.bfloat16
NN = ((1,), (0,))
NT = ((1,), (1,))
TN = ((0,), (0,))

NX, NZ, NY, NC = 4, 8, 4, 2
COUNT = 512
STEP = 64
BLOCKS = [(i, j) for i in range(4) for j in range(i + 1)]


def shift_x(k):
    return [(z * NX + x, z * NX + (x + k) % NX) for z in range(NZ) for x in range(NX)]


def shift_z(k):
    return [(z * NX + x, (z + k) % NZ * NX + x) for z in range(NZ) for x in range(NX)]


def shift_y(k):
    return [(y * NC + c, (y + k) % NY * NC + c) for y in range(NY) for c in range(NC)]


SWAP = [(y * NC + c, y * NC + 1 - c) for y in range(NY) for c in range(NC)]


def place():
    row, layer = lax.axis_index("row"), lax.axis_index("layer")
    return row // NX, lax.rem(row, NX), layer // NC, lax.rem(layer, NC)


def matern(first_points, second_points):
    first_float = first_points.astype(F32)
    second_float = second_points.astype(F32)
    delta_x = first_float[0][:, None] - second_float[0][None, :]
    delta_y = first_float[1][:, None] - second_float[1][None, :]
    scaled = jnp.sqrt(delta_x * delta_x + delta_y * delta_y) * (jnp.sqrt(3.0) / length_scale)
    return variance_value * (1.0 + scaled) * jnp.exp(-scaled)


def product(a, b, dims):
    return lax.dot_general(a, b, (dims, ((), ())), precision=lax.Precision.HIGHEST, preferred_element_type=F32)


def upper_lower(a):
    up = a.astype(BF16)
    return up, (a - up.astype(F32)).astype(BF16)


def halves_product(a_up, a_low, b):
    one = lambda u, v: lax.dot_general(u, v, (NT, ((), ())), preferred_element_type=F32)
    b_up, b_low = upper_lower(b)
    return one(a_low, b_up) + one(a_up, b_low) + one(a_up, b_up)


VMEM = pl.BlockSpec(memory_space=pltpu.VMEM)


def grant(mib):
    return pltpu.CompilerParams(vmem_limit_bytes=mib << 20)


PIECES = ((0, 0), (-1, 0), (1, 0), (-2, 0), (2, 0), (-3, 0), (3, 0), (4, 0), (4, 2))


def tower(own):
    hop = lambda a, k: lax.ppermute(a, "row", shift_z(k))
    up1, down1, up2, down2 = hop(own, 1), hop(own, -1), hop(own, 2), hop(own, -2)
    up3, down3 = hop(up2, 1), hop(down2, -1)
    up4, down4 = hop(up2[:32], 2), hop(down2[32:], -2)
    return [own, up1, down1, up2, down2, up3, down3, up4, down4]


def gram_kernel(*refs):
    pieces, (rows, sides, other, mine, blocks) = refs[:9], refs[9:]
    z, x, y, c = place()
    for piece, (turn, first) in zip(pieces, PIECES):

        @pl.loop(0, piece.shape[0] // 16)
        def _(i):
            at = (lax.rem(z + turn + NZ, NZ) * NX + lax.rem(x - first - i + NX, NX)) * 16
            at = pl.ds(pl.multiple_of(at, 16), 16)
            held = piece[pl.ds(pl.multiple_of(16 * i, 16), 16)]
            rows[at] = held[:, :2048]
            sides[at] = held[:, 2048:]

    at = 0
    for i in range(4):
        part = lax.dot_general(
            rows[128 * i : 128 * i + 128], rows[: 128 * i + 128], (NT, ((), ())), preferred_element_type=F32
        )
        for j in range(i + 1):
            blocks[at] = part[:, 128 * j : 128 * j + 128]
            at += 1
    for k in range(NY):
        for out, core in ((other, 1 - c), (mine, c)):
            first = pl.multiple_of(64 * core + 16 * lax.rem(y + k, NY), 16)
            for b in range(len(BLOCKS)):
                out[k, 16 * b : 16 * b + 16] = blocks[b, pl.ds(first, 16), :]


def gram(pieces):
    chunk = jax.ShapeDtypeStruct((NY, 16 * len(BLOCKS), 128), F32)
    return pl.pallas_call(
        gram_kernel,
        name="gram",
        out_shape=(
            jax.ShapeDtypeStruct((COUNT, 2048), BF16),
            jax.ShapeDtypeStruct((COUNT, 128), BF16),
            chunk,
            chunk,
        ),
        in_specs=[VMEM] * 9,
        out_specs=(VMEM,) * 4,
        scratch_shapes=[pltpu.VMEM((len(BLOCKS), 128, 128), F32)],
        compiler_params=grant(10),
        cost_estimate=pl.CostEstimate(flops=2 * COUNT * COUNT * 2048, bytes_accessed=2 << 20, transcendentals=0),
    )(*pieces)


def schur_kernel(window, rows, other, mine, held, sem):
    _, _, y, c = place()

    def fetch(i):
        slot = lax.rem(i, 2)
        core = jnp.where(i < 2, 1 - c, c)
        first = pl.multiple_of(512 * core + 256 * slot, 256)
        return pltpu.make_async_copy(window.at[pl.ds(first, 256)], held.at[slot], sem.at[slot])

    fetch(0).start()

    @pl.loop(0, 4)
    def _(i):
        @pl.when(i < 3)
        def _():
            fetch(i + 1).start()

        fetch(i).wait()
        part = lax.dot_general(held[lax.rem(i, 2)], rows[...], (NT, ((), ())), preferred_element_type=F32)
        for n in range(2):
            k = lax.rem(2 * lax.rem(i, 2) + n - y + NY, NY)

            @pl.when(i < 2)
            def _():
                other[k] = part[128 * n : 128 * n + 128]

            @pl.when(i >= 2)
            def _():
                mine[k] = part[128 * n : 128 * n + 128]


def schur(window, rows):
    chunk = jax.ShapeDtypeStruct((NY, 128, COUNT), F32)
    return pl.pallas_call(
        schur_kernel,
        name="schur",
        out_shape=(chunk, chunk),
        in_specs=[pl.BlockSpec(memory_space=pltpu.HBM), VMEM],
        out_specs=(VMEM, VMEM),
        scratch_shapes=[pltpu.VMEM((2, 256, 2048), BF16), pltpu.SemaphoreType.DMA((2,))],
        compiler_params=grant(12),
        cost_estimate=pl.CostEstimate(flops=2 * 1024 * COUNT * 2048, bytes_accessed=8 << 20, transcendentals=0),
    )(window, rows)


def tree_sum(terms):
    terms = list(terms)
    while len(terms) > 1:
        terms = [terms[i] + terms[i + 1] if i + 1 < len(terms) else terms[i] for i in range(0, len(terms), 2)]
    return terms[0]


def invert_factor(block):
    lane = lax.broadcasted_iota(jnp.int32, (STEP, STEP), 1)
    sub = lax.broadcasted_iota(jnp.int32, (STEP, STEP), 0)
    both = jnp.concatenate([block, jnp.where(lane == sub, 1.0, 0.0).astype(F32)], axis=1)
    a = [both[8 * g : 8 * g + 8] for g in range(8)]
    row = lax.broadcasted_iota(jnp.int32, (8, 128), 0)
    spread = lambda v, j: jnp.broadcast_to(v[j : j + 1], (8, 128))
    lanes = lambda v, j: jnp.broadcast_to(v[:, j : j + 1], (8, 128))
    done = []
    column = [lanes(a[0], c) for c in range(8)]
    for p in range(8):
        more = p + 1 < 8
        if more:
            below = [lanes(a[p + 1], 8 * p + 8 + c) for c in range(8)]
            right = [lanes(a[p], 8 * p + 8 + c) for c in range(8)]
        old = {(c, g): lanes(a[g], 8 * p + c) for g in range(p + 1, 8) for c in range(8)}
        factor_rows = solved_rows = a[p]
        pivots = jnp.ones((8, 128), F32)
        scale = pivots
        for j in range(8):
            d = spread(column[j], j)
            r = 1.0 / d
            full = jnp.where(row != j, column[j], 0.0)
            low = jnp.where(row > j, column[j], 0.0)
            full_r = full * r
            lead = spread(factor_rows, j) * r
            for c in range(j + 1, 8):
                if c == j + 1:
                    column[c] = column[c] - (full * spread(column[c], j)) * r
                else:
                    column[c] = column[c] - full_r * spread(column[c], j)
            if more:
                right = [v - full_r * spread(v, j) for v in right]
            solved_rows = solved_rows - full * lead
            factor_rows = factor_rows - low * lead
            pivots = jnp.where(row == j, d, pivots)
            scale = jnp.where(row == j, r, scale)
        done.append(factor_rows * lax.rsqrt(pivots))
        if more:
            right = [v * scale for v in right]
            column = [below[c] - tree_sum(old[k, p + 1] * spread(right[c], k) for k in range(8)) for c in range(8)]
        solved_rows = solved_rows * scale
        heads = [spread(solved_rows, c) for c in range(8)]
        for g in range(p + 1, 8):
            a[g] = a[g] - tree_sum(old[c, g] * heads[c] for c in range(8))
    return jnp.concatenate(done, axis=0)[:, STEP:]


def factor_steps(a, e, block, half, cross, first):
    b, w = STEP, 128

    def upper(k):
        lo = k * w
        mid, hi = lo + b, lo + w
        t1 = half[...]
        inner = product(a[mid:hi, lo:mid], t1, NT)
        block[...] = a[mid:hi, mid:hi] - product(inner, inner, NT)
        e[lo:mid, lo:mid] = t1
        cross[...] = product(inner, t1, NN)

    def lower(k):
        lo = k * w
        mid, hi, nx = lo + b, lo + w, lo + 2 * w
        t2 = half[...]
        e[mid:hi, lo:mid] = -product(t2, cross[...], NN)
        e[mid:hi, mid:hi] = t2
        t = e[lo:hi, lo:hi]
        if hi < COUNT:
            below = product(a[hi:nx, lo:hi], t, NT)
            square = a[hi:nx, hi:nx] - product(below, below, NT)
            a[hi:nx, hi:nx] = square
            block[...] = square[:b, :b]
        if k > 0:
            left = product(t, e[lo:hi, :lo], NN)
            e[lo:hi, :lo] = left
        if hi < COUNT:
            if k > 0:
                e[hi:nx, :lo] = e[hi:nx, :lo] - product(below, left, NN)
            e[hi:nx, lo:hi] = -product(below, t, NN)
            if nx < COUNT:
                rest = product(a[nx:, lo:hi], t, NT)
                a[nx:, hi:nx] = a[nx:, hi:nx] - product(rest, below, NT)
                a[nx:, nx:] = a[nx:, nx:] - product(rest, rest, NT)
                if k > 0:
                    e[nx:, :lo] = e[nx:, :lo] - product(rest, left, NN)
                e[nx:, lo:hi] = -product(rest, t, NN)

    @pl.loop(0, 4)
    def _(i):
        half[...] = invert_factor(block[...])
        for n, (part, k) in enumerate(((upper, first), (lower, first), (upper, first + 1), (lower, first + 1))):
            pl.when(i == n)(lambda part=part, k=k: part(k))


STEPS_SCRATCH = [pltpu.VMEM((STEP, STEP), F32)] * 3


def factor_kernel(cov, own, near1, near2, near3, far, a, e, block, half, cross):
    _, _, y, c = place()
    for k in range(NY):
        for core in range(NC):
            piece = (own, near1, near2, near3)[k] if core == 0 else far.at[k]
            which = c if core == 0 else 1 - c
            first = pl.multiple_of(64 * which + 16 * lax.rem(y - k + NY, NY), 16)
            for b, (i, j) in enumerate(BLOCKS):
                at = (pl.ds(128 * i + first, 16), slice(128 * j, 128 * j + 128))
                a[at] = cov[at] - piece[16 * b : 16 * b + 16]
    e[...] = jnp.zeros_like(e)
    block[...] = a[:STEP, :STEP]
    factor_steps(a, e, block, half, cross, 0)


def factor(*args):
    square = jax.ShapeDtypeStruct((COUNT, COUNT), F32)
    return pl.pallas_call(
        factor_kernel,
        name="factor",
        out_shape=(square, square),
        in_specs=[VMEM] * 6,
        out_specs=(VMEM, VMEM),
        scratch_shapes=STEPS_SCRATCH,
        compiler_params=grant(10),
        cost_estimate=pl.CostEstimate(flops=10**10, bytes_accessed=4 << 20, transcendentals=0),
    )(*args)


def weights_kernel(a_in, e_in, sides, a, e, weights, block, half, cross):
    layer = lax.axis_index("layer")
    block[...] = a[256 : 256 + STEP, 256 : 256 + STEP]
    factor_steps(a, e, block, half, cross, 2)
    reduced = product(e[...], sides[:, :64].astype(F32), NN)
    weights[:64] = e[pl.ds(pl.multiple_of(64 * layer, 64), 64), :]
    weights[64:] = product(reduced, e[...], TN)


def weigh(a, e, sides):
    square = jax.ShapeDtypeStruct((COUNT, COUNT), F32)
    return pl.pallas_call(
        weights_kernel,
        name="weigh",
        out_shape=(square, square, jax.ShapeDtypeStruct((128, COUNT), F32)),
        in_specs=[VMEM] * 3,
        out_specs=(VMEM,) * 3,
        scratch_shapes=STEPS_SCRATCH,
        input_output_aliases={0: 0, 1: 1},
        compiler_params=grant(10),
        cost_estimate=pl.CostEstimate(flops=10**10, bytes_accessed=4 << 20, transcendentals=0),
    )(a, e, sides)[2]


def finish_kernel(weights, near, far, sides, panel, rest):
    _, _, y, c = place()
    up, low = upper_lower(weights[...])
    for piece, core in ((near, c), (far, 1 - c)):
        for k in range(NY):
            at = pl.multiple_of(512 * core + 128 * lax.rem(y - k + NY, NY), 128)
            both = halves_product(up, low, piece[k])
            panel[:, pl.ds(at, 128)] = both[:64]
            rest[:, pl.ds(at, 128)] = sides[:, pl.ds(at, 128)].astype(F32) - both[64:]


def finish(*args):
    return pl.pallas_call(
        finish_kernel,
        name="finish",
        out_shape=(jax.ShapeDtypeStruct((64, 1024), F32),) * 2,
        in_specs=[VMEM] * 4,
        out_specs=(VMEM, VMEM),
        compiler_params=grant(12),
        cost_estimate=pl.CostEstimate(flops=6 * 1024 * 512 * 128, bytes_accessed=3 << 20, transcendentals=0),
    )(*args)


def shards(window_points, pivot_points, window_factor, pivot_factor, right_sides, pivot_sides):
    _, _, y, c = place()
    swap = lambda a: lax.ppermute(a, "layer", SWAP)
    along = lambda a, k: lax.ppermute(a, "layer", shift_y(k))

    held = jnp.concatenate([pivot_factor, pivot_sides, jnp.zeros_like(pivot_sides)], axis=1)
    near = [held] + [lax.ppermute(held, "row", shift_x(k)) for k in (1, 2, 3)]
    pieces = tower(jnp.concatenate(near, axis=0))
    rows, sides, gram_other, gram_mine = gram(pieces)
    gram_far = swap(gram_other)
    gram_sum = [gram_mine[k] + gram_far[k] for k in range(NY)]
    gram_in = [along(gram_sum[k], k) for k in (1, 2, 3)]
    gram_own = gram_sum[0] + (gram_in[0] + gram_in[1] + gram_in[2])
    gram_near = [gram_own] + [along(gram_own, k) for k in (1, 2, 3)]
    gram_far = swap(jnp.stack(gram_near))

    points = lax.dynamic_slice_in_dim(window_points, 512 * c + 128 * y, 128, 1)
    cov = matern(pivot_points, pivot_points) + nugget_value * jnp.eye(COUNT, dtype=F32)
    covered = matern(points, pivot_points)
    cov, covered = lax.optimization_barrier((cov, covered))
    a, e = factor(cov, *gram_near, gram_far)
    weights = weigh(a, e, sides)

    schur_other, schur_mine = schur(window_factor, rows)
    schur_far = swap(schur_other)
    schur_sum = [schur_mine[k] + schur_far[k] for k in range(NY)]
    schur_in = [along(schur_sum[k], k) for k in (1, 2, 3)]
    panel_own = covered - (schur_sum[0] + (schur_in[0] + schur_in[1] + schur_in[2]))
    panel_near = jnp.stack([panel_own] + [along(panel_own, k) for k in (1, 2, 3)])
    panel_far = swap(panel_near)
    panel, rest = finish(weights, panel_near, panel_far, right_sides.T)
    return panel.T, rest.T


def solution(mesh):
    placed = (
        P(None, "row"),
        P(),
        P("row", "layer"),
        P("row", "layer"),
        P("row", "layer"),
        P("row", "layer"),
    )
    return jax.shard_map(
        shards,
        mesh=mesh,
        in_specs=placed,
        out_specs=(P("row", "layer"), P("row", "layer")),
        check_vma=False,
    )
```

profile of v0, /device:TPU:1, one launch (start us, length us, event | category | flops | bytes accessed | tf_op | source)
XLA Modules:
  0.0 122.3 jit_solution(6442374361718504224)
XLA Ops:
  0.6 0.9 concatenate.6
  1.6 2.1 %collective-permute-start = (bf16[16,2176]{1,0:T(8,128)(2,1)S(1)}, bf16[16,2176]{1,0:T(8,128)(2,1)S(1)}, u32[]{:S(2)}, u32[]{:S(2)}) collective-permute-start(bf16[16,2176]{1,0:T(8,128)(2,1)S(1)} %concatenate.6), channel_id=1, source_target_pairs={{0,8},{8,16},{16,24},{24,0},{32,40},{40,48},{48,56},{56,32},{64,72... | collective-permute-start | bytes 208904 | tf_op jit(solution)/shard_map/ppermute | solution.py:366
  3.6 2.5 %collective-permute-start.1 = (bf16[16,2176]{1,0:T(8,128)(2,1)S(1)}, bf16[16,2176]{1,0:T(8,128)(2,1)S(1)}, u32[]{:S(2)}, u32[]{:S(2)}) collective-permute-start(bf16[16,2176]{1,0:T(8,128)(2,1)S(1)} %concatenate.6), channel_id=1, source_target_pairs={{0,16},{8,24},{16,0},{24,8},{32,48},{40,56},{48,32},{56,40},{64,80... | collective-permute-start | bytes 208904 | tf_op jit(solution)/shard_map/ppermute | solution.py:366
  6.1 1.2 collective-permute-start.2
  7.2 0.0 collective-permute-done
  7.2 1.6 %collective-permute-done.1 = bf16[16,2176]{1,0:T(8,128)(2,1)S(1)} collective-permute-done((bf16[16,2176]{1,0:T(8,128)(2,1)S(1)}, bf16[16,2176]{1,0:T(8,128)(2,1)S(1)}, u32[]{:S(2)}, u32[]{:S(2)}) %collective-permute-start.1) | collective-permute-done | bytes 69664 | tf_op jit(solution)/shard_map/ppermute | solution.py:366
  8.9 0.7 collective-permute-done.2
  9.6 3.4 %collective-permute-start.5 = (bf16[64,2176]{1,0:T(8,128)(2,1)S(1)}, bf16[64,2176]{1,0:T(8,128)(2,1)S(1)}, u32[]{:S(2)}, u32[]{:S(2)}) collective-permute-start(bf16[64,2176]{1,0:T(8,128)(2,1)S(1)} %pad_maximum_fusion.2.refs_0_), channel_id=1, source_target_pairs={{0,64},{8,72},{16,80},{24,88},{32,96},{40,104},{48,112},{56,120},{... | collective-permute-start | bytes 835592 | tf_op jit(solution)/shard_map/ppermute | solution.py:81
  12.9 3.1 %collective-permute-start.6 = (bf16[64,2176]{1,0:T(8,128)(2,1)S(1)}, bf16[64,2176]{1,0:T(8,128)(2,1)S(1)}, u32[]{:S(2)}, u32[]{:S(2)}) collective-permute-start(bf16[64,2176]{1,0:T(8,128)(2,1)S(1)} %pad_maximum_fusion.2.refs_0_), channel_id=1, source_target_pairs={{0,192},{8,200},{16,208},{24,216},{32,224},{40,232},{48,240},{56,2... | collective-permute-start | bytes 835592 | tf_op jit(solution)/shard_map/ppermute | solution.py:81
  16.0 0.7 collective-permute-start.3
  16.8 1.9 %collective-permute-start.4 = (bf16[64,2176]{1,0:T(8,128)(2,1)S(1)}, bf16[64,2176]{1,0:T(8,128)(2,1)S(1)}, u32[]{:S(2)}, u32[]{:S(2)}) collective-permute-start(bf16[64,2176]{1,0:T(8,128)(2,1)S(1)} %pad_maximum_fusion.2.refs_0_), channel_id=1, source_target_pairs={{0,224},{8,232},{16,240},{24,248},{32,0},{40,8},{48,16},{56,24},{6... | collective-permute-start | bytes 835592 | tf_op jit(solution)/shard_map/ppermute | solution.py:81
  18.7 4.3 %collective-permute-done.5.refs_3_ = bf16[64,2176]{1,0:T(8,128)(2,1)S(1)} collective-permute-done((bf16[64,2176]{1,0:T(8,128)(2,1)S(1)}, bf16[64,2176]{1,0:T(8,128)(2,1)S(1)}, u32[]{:S(2)}, u32[]{:S(2)}) %collective-permute-start.5) | collective-permute-done | bytes 278560 | tf_op jit(solution)/shard_map/ppermute | solution.py:81
  23.1 5.4 %collective-permute-start.7 = (bf16[64,2176]{1,0:T(8,128)(2,1)S(1)}, bf16[64,2176]{1,0:T(8,128)(2,1)S(1)}, u32[]{:S(2)}, u32[]{:S(2)}) collective-permute-start(bf16[64,2176]{1,0:T(8,128)(2,1)S(1)} %collective-permute-done.5.refs_3_), channel_id=1, source_target_pairs={{0,32},{8,40},{16,48},{24,56},{32,64},{40,72},{48,80},{56,88},{64,... | collective-permute-start | bytes 835592 | tf_op jit(solution)/shard_map/ppermute | solution.py:81
  28.5 0.8 collective-permute-done.6.refs_4_
  29.3 0.0 collective-permute-start.8
  29.3 1.5 %collective-permute-start.10 = (bf16[32,2176]{1,0:T(8,128)(2,1)S(1)}, bf16[32,2176]{1,0:T(8,128)(2,1)S(1)}, u32[]{:S(2)}, u32[]{:S(2)}) collective-permute-start(bf16[32,2176]{1,0:T(8,128)(2,1)S(1)} %slice.95), channel_id=1, source_target_pairs={{0,192},{8,200},{16,208},{24,216},{32,224},{40,232},{48,240},{56,2... | collective-permute-start | bytes 417800 | tf_op jit(solution)/shard_map/ppermute | solution.py:81
  30.8 3.3 %collective-permute-done.3.refs_1_ = bf16[64,2176]{1,0:T(8,128)(2,1)S(1)} collective-permute-done((bf16[64,2176]{1,0:T(8,128)(2,1)S(1)}, bf16[64,2176]{1,0:T(8,128)(2,1)S(1)}, u32[]{:S(2)}, u32[]{:S(2)}) %collective-permute-start.3) | collective-permute-done | bytes 278560 | tf_op jit(solution)/shard_map/ppermute | solution.py:81
  34.1 0.0 collective-permute-start.9
  34.1 0.1 collective-permute-done.4.refs_2_
  34.2 13.4 %collective-permute-done.10.refs_8_ = bf16[32,2176]{1,0:T(8,128)(2,1)S(1)} collective-permute-done((bf16[32,2176]{1,0:T(8,128)(2,1)S(1)}, bf16[32,2176]{1,0:T(8,128)(2,1)S(1)}, u32[]{:S(2)}, u32[]{:S(2)}) %collective-permute-start.10) | collective-permute-done | bytes 139296 | tf_op jit(solution)/shard_map/ppermute | solution.py:81
  47.6 0.0 collective-permute-done.9.refs_7_
  47.6 0.0 collective-permute-done.7.refs_5_
  47.6 0.0 collective-permute-done.8.refs_6_
  47.6 2.2 %gram.1 = (bf16[512,2048]{1,0:T(8,128)(2,1)S(1)}, bf16[512,128]{1,0:T(8,128)(2,1)S(1)}, f32[4,160,128]{2,1,0:T(8,128)S(1)}, f32[4,160,128]{2,1,0:T(8,128)S(1)}) custom-call(bf16[64,2176]{1,0:T(8,128)(2,1)S(1)} %pad_maximum_fusion.2.refs_0_, bf16[64,2176]{1,0:T(8,128)(2,1)S(1)} %collective-permute-done.3.refs_1_, ...), custom_call_target="tpu_custom_call" | custom-call | flops 1073741824 | bytes 2097152 | tf_op jit(solution)/shard_map/gram/pallas_call | solution.py:118
  49.8 0.0 copy-start.2
  49.8 3.5 %schur.1 = (f32[4,128,512]{2,1,0:T(8,128)S(1)}, f32[4,128,512]{2,1,0:T(8,128)S(1)}) custom-call(bf16[1024,2048]{1,0:T(8,128)(2,1)S(1)} %copy-done.1, bf16[512,2048]{1,0:T(8,128)(2,1)S(1)} %get-tuple-element.23.rows), custom_call_target="tpu_custom_call" | custom-call | flops 2147483648 | bytes 8388608 | tf_op jit(solution)/shard_map/schur/pallas_call | solution.py:168
  53.3 1.1 collective-permute-start.19
  54.4 0.7 dynamic-slice_convert_fusion
  55.1 0.1 collective-permute-start.11
  55.2 0.7 select_add_fusion.cov
  55.9 1.3 %collective-permute-done.11 = f32[4,160,128]{2,1,0:T(8,128)S(1)} collective-permute-done((f32[4,160,128]{2,1,0:T(8,128)S(1)}, f32[4,160,128]{2,1,0:T(8,128)S(1)}, u32[]{:S(2)}, u32[]{:S(2)}) %collective-permute-start.11) | collective-permute-done | bytes 327712 | tf_op jit(solution)/shard_map/ppermute | solution.py:362
  57.2 1.6 %collective-permute-start.12 = (f32[160,128]{1,0:T(8,128)S(1)}, f32[160,128]{1,0:T(8,128)S(1)}, u32[]{:S(2)}, u32[]{:S(2)}) collective-permute-start(f32[160,128]{1,0:T(8,128)S(1)} %get-tuple-element.33), channel_id=1, source_target_pairs={{0,2},{1,3},{2,4},{3,5},{4,6},{5,7},{6,0},{7,1},{8,10},{9,11},{10,... | collective-permute-start | bytes 245768 | tf_op jit(solution)/shard_map/ppermute | solution.py:363
  58.8 2.6 %collective-permute-start.13 = (f32[160,128]{1,0:T(8,128)S(1)}, f32[160,128]{1,0:T(8,128)S(1)}, u32[]{:S(2)}, u32[]{:S(2)}) collective-permute-start(f32[160,128]{1,0:T(8,128)S(1)} %get-tuple-element.31), channel_id=1, source_target_pairs={{0,4},{1,5},{2,6},{3,7},{4,0},{5,1},{6,2},{7,3},{8,12},{9,13},{10,... | collective-permute-start | bytes 245768 | tf_op jit(solution)/shard_map/ppermute | solution.py:363
  61.4 1.1 collective-permute-start.14
  62.5 0.0 collective-permute-done.19
  62.5 1.2 %fusion.1 = (f32[128,512]{1,0:T(8,128)S(1)}, f32[128,512]{1,0:T(8,128)S(1)}, f32[128,512]{1,0:T(8,128)S(1)}) fusion(f32[4,128,512]{2,1,0:T(8,128)} %collective-permute-done.19, f32[4,128,512]{2,1,0:T(8,128)S(1)} %get-tuple-element.24), kind=kLoop, calls=%fused_computation.8 | loop fusion | flops 196608 | bytes 2359296 | tf_op jit(solution)/shard_map/add | solution.py:385
  63.7 0.5 collective-permute-start.20
  64.2 0.8 collective-permute-start.21
  65.0 0.0 collective-permute-done.12
  65.0 1.7 %collective-permute-start.22 = (f32[128,512]{1,0:T(8,128)S(1)}, f32[128,512]{1,0:T(8,128)S(1)}, u32[]{:S(2)}, u32[]{:S(2)}) collective-permute-start(f32[128,512]{1,0:T(8,128)S(1)} %get-tuple-element.29), channel_id=1, source_target_pairs={{0,6},{1,7},{2,0},{3,1},{4,2},{5,3},{6,4},{7,5},{8,14},{9,15},{10,... | collective-permute-start | bytes 786440 | tf_op jit(solution)/shard_map/ppermute | solution.py:363
  66.7 0.2 exponential_multiply_fusion
  66.9 0.0 collective-permute-done.13
  67.0 2.2 %collective-permute-start.16 = (f32[160,128]{1,0:T(8,128)S(1)}, f32[160,128]{1,0:T(8,128)S(1)}, u32[]{:S(2)}, u32[]{:S(2)}) collective-permute-start(f32[160,128]{1,0:T(8,128)S(1)} %fusion.10.own), channel_id=1, source_target_pairs={{0,4},{1,5},{2,6},{3,7},{4,0},{5,1},{6,2},{7,3},{8,12},{9,13},{10,... | collective-permute-start | bytes 245768 | tf_op jit(solution)/shard_map/ppermute | solution.py:363
  69.2 0.6 collective-permute-start.17
  69.8 3.0 %collective-permute-done.20 = f32[128,512]{1,0:T(8,128)S(1)} collective-permute-done((f32[128,512]{1,0:T(8,128)S(1)}, f32[128,512]{1,0:T(8,128)S(1)}, u32[]{:S(2)}, u32[]{:S(2)}) %collective-permute-start.20) | collective-permute-done | bytes 262176 | tf_op jit(solution)/shard_map/ppermute | solution.py:363
  72.9 0.0 collective-permute-start.15
  72.9 3.2 %collective-permute-done.21 = f32[128,512]{1,0:T(8,128)S(1)} collective-permute-done((f32[128,512]{1,0:T(8,128)S(1)}, f32[128,512]{1,0:T(8,128)S(1)}, u32[]{:S(2)}, u32[]{:S(2)}) %collective-permute-start.21) | collective-permute-done | bytes 262176 | tf_op jit(solution)/shard_map/ppermute | solution.py:363
  76.1 2.9 %collective-permute-done.22 = f32[128,512]{1,0:T(8,128)S(1)} collective-permute-done((f32[128,512]{1,0:T(8,128)S(1)}, f32[128,512]{1,0:T(8,128)S(1)}, u32[]{:S(2)}, u32[]{:S(2)}) %collective-permute-start.22) | collective-permute-done | bytes 262176 | tf_op jit(solution)/shard_map/ppermute | solution.py:363
  79.0 1.1 fusion.5
  80.1 1.6 %collective-permute-start.23 = (f32[128,512]{1,0:T(8,128)S(1)}, f32[128,512]{1,0:T(8,128)S(1)}, u32[]{:S(2)}, u32[]{:S(2)}) collective-permute-start(f32[128,512]{1,0:T(8,128)S(1)} %fusion.5), channel_id=1, source_target_pairs={{0,2},{1,3},{2,4},{3,5},{4,6},{5,7},{6,0},{7,1},{8,10},{9,11},{10,... | collective-permute-start | bytes 786440 | tf_op jit(solution)/shard_map/ppermute | solution.py:363
  81.7 3.2 %collective-permute-start.24 = (f32[128,512]{1,0:T(8,128)S(1)}, f32[128,512]{1,0:T(8,128)S(1)}, u32[]{:S(2)}, u32[]{:S(2)}) collective-permute-start(f32[128,512]{1,0:T(8,128)S(1)} %fusion.5), channel_id=1, source_target_pairs={{0,4},{1,5},{2,6},{3,7},{4,0},{5,1},{6,2},{7,3},{8,12},{9,13},{10,... | collective-permute-start | bytes 786440 | tf_op jit(solution)/shard_map/ppermute | solution.py:363
  84.9 0.0 collective-permute-done.15.near1
  85.0 3.7 %collective-permute-start.18 = (f32[4,160,128]{2,1,0:T(8,128)S(1)}, f32[4,160,128]{2,1,0:T(8,128)S(1)}, u32[]{:S(2)}, u32[]{:S(2)}) collective-permute-start(f32[4,160,128]{2,1,0:T(8,128)S(1)} %pad_maximum_fusion.1), channel_id=1, source_target_pairs={{0,1},{1,0},{2,3},{3,2},{4,5},{5,4},{6,7},{7,6},{8,9},{9,8},{10,11... | collective-permute-start | bytes 983048 | tf_op jit(solution)/shard_map/ppermute | solution.py:362
  88.6 0.9 collective-permute-done.23
  89.5 4.7 %collective-permute-done.24 = f32[128,512]{1,0:T(8,128)S(1)} collective-permute-done((f32[128,512]{1,0:T(8,128)S(1)}, f32[128,512]{1,0:T(8,128)S(1)}, u32[]{:S(2)}, u32[]{:S(2)}) %collective-permute-start.24) | collective-permute-done | bytes 262176 | tf_op jit(solution)/shard_map/ppermute | solution.py:363
  94.2 1.0 collective-permute-done.25
  95.3 0.1 pad_maximum_fusion.near
  95.3 2.8 %collective-permute-start.26 = (f32[4,128,512]{2,1,0:T(8,128)S(1)}, f32[4,128,512]{2,1,0:T(8,128)S(1)}, u32[]{:S(2)}, u32[]{:S(2)}) collective-permute-start(f32[4,128,512]{2,1,0:T(8,128)S(1)} %pad_maximum_fusion.near), channel_id=1, source_target_pairs={{0,1},{1,0},{2,3},{3,2},{4,5},{5,4},{6,7},{7,6},{8,9},{9,8},{10,11... | collective-permute-start | bytes 3145736 | tf_op jit(solution)/shard_map/ppermute | solution.py:362
  98.2 0.0 collective-permute-done.18.far
  98.2 10.9 %factor.1 = (f32[512,512]{1,0:T(8,128)S(1)}, f32[512,512]{1,0:T(8,128)S(1)}) custom-call(f32[512,512]{1,0:T(8,128)S(1)} %select_add_fusion.cov, f32[160,128]{1,0:T(8,128)S(1)} %fusion.10.own, f32[160,128]{1,0:T(8,128)S(1)} %collective-permute-done.15.near1, f32[160,128]{1,0:T(8,128)S(1)} %collective-permute-done.16.near2, ...), custom_call_target="tpu_custom_call" | custom-call | flops 10000000000 | bytes 4194304 | tf_op jit(solution)/shard_map/factor/pallas_call | solution.py:301
  109.1 0.0 copy-start
  109.1 11.3 %weigh.1 = (f32[512,512]{1,0:T(8,128)S(1)}, f32[512,512]{1,0:T(8,128)S(1)}, f32[128,512]{1,0:T(8,128)S(1)}) custom-call(f32[512,512]{1,0:T(8,128)S(1)} %get-tuple-element.18.a_in, f32[512,512]{1,0:T(8,128)S(1)} %get-tuple-element.19.e_in, bf16[512,128]{1,0:T(8,128)(2,1)S(1)} %get-tuple-element.20.sides), custom_call_target="tpu_custom_call", output_to_operand_aliasing={{0}: (0, {}), {1}: (1, {})} | custom-call | flops 10000000000 | bytes 4194304 | tf_op jit(solution)/shard_map/weigh/pallas_call | solution.py:324
  120.5 0.0 collective-permute-done.26.far
  120.5 1.8 %finish.1 = (f32[64,1024]{1,0:T(8,128)}, f32[64,1024]{1,0:T(8,128)}) custom-call(f32[128,512]{1,0:T(8,128)S(1)} %get-tuple-element.21.weights, f32[4,128,512]{2,1,0:T(8,128)S(1)} %pad_maximum_fusion.near, f32[4,128,512]{2,1,0:T(8,128)S(1)} %collective-permute-done.26.far, bf16[64,1024]{1,0:T(8,128)(2,1)S(1)} %bitcast.40), custom_call_target="tpu_custom_call" | custom-call | flops 402653184 | bytes 3145728 | tf_op jit(solution)/shard_map/finish/pallas_call | solution.py:349
  (18 shorter events, 0.2 us)
Async XLA Ops:
  1.6 48.3 %copy-start.1 = (bf16[1024,2048]{1,0:T(8,128)(2,1)S(1)}, bf16[1024,2048]{1,0:T(8,128)(2,1)}, u32[]{:S(2)}) copy-start(bf16[1024,2048]{1,0:T(8,128)(2,1)} %window.1) | copy-start | bytes 12582916
  1.6 5.7 %collective-permute-start = (bf16[16,2176]{1,0:T(8,128)(2,1)S(1)}, bf16[16,2176]{1,0:T(8,128)(2,1)S(1)}, u32[]{:S(2)}, u32[]{:S(2)}) collective-permute-start(bf16[16,2176]{1,0:T(8,128)(2,1)S(1)} %concatenate.6), channel_id=1, source_target_pairs={{0,8},{8,16},{16,24},{24,0},{32,40},{40,48},{48,56},{56,32},{64,72... | collective-permute-start | bytes 208904 | tf_op jit(solution)/shard_map/ppermute | solution.py:366
  3.6 5.2 %collective-permute-start.1 = (bf16[16,2176]{1,0:T(8,128)(2,1)S(1)}, bf16[16,2176]{1,0:T(8,128)(2,1)S(1)}, u32[]{:S(2)}, u32[]{:S(2)}) collective-permute-start(bf16[16,2176]{1,0:T(8,128)(2,1)S(1)} %concatenate.6), channel_id=1, source_target_pairs={{0,16},{8,24},{16,0},{24,8},{32,48},{40,56},{48,32},{56,40},{64,80... | collective-permute-start | bytes 208904 | tf_op jit(solution)/shard_map/ppermute | solution.py:366
  6.1 3.5 %collective-permute-start.2 = (bf16[16,2176]{1,0:T(8,128)(2,1)S(1)}, bf16[16,2176]{1,0:T(8,128)(2,1)S(1)}, u32[]{:S(2)}, u32[]{:S(2)}) collective-permute-start(bf16[16,2176]{1,0:T(8,128)(2,1)S(1)} %concatenate.6), channel_id=1, source_target_pairs={{0,24},{8,0},{16,8},{24,16},{32,56},{40,32},{48,40},{56,48},{64,88... | collective-permute-start | bytes 208904 | tf_op jit(solution)/shard_map/ppermute | solution.py:366
  9.6 13.5 %collective-permute-start.5 = (bf16[64,2176]{1,0:T(8,128)(2,1)S(1)}, bf16[64,2176]{1,0:T(8,128)(2,1)S(1)}, u32[]{:S(2)}, u32[]{:S(2)}) collective-permute-start(bf16[64,2176]{1,0:T(8,128)(2,1)S(1)} %pad_maximum_fusion.2.refs_0_), channel_id=1, source_target_pairs={{0,64},{8,72},{16,80},{24,88},{32,96},{40,104},{48,112},{56,120},{... | collective-permute-start | bytes 835592 | tf_op jit(solution)/shard_map/ppermute | solution.py:81
  12.9 16.3 %collective-permute-start.6 = (bf16[64,2176]{1,0:T(8,128)(2,1)S(1)}, bf16[64,2176]{1,0:T(8,128)(2,1)S(1)}, u32[]{:S(2)}, u32[]{:S(2)}) collective-permute-start(bf16[64,2176]{1,0:T(8,128)(2,1)S(1)} %pad_maximum_fusion.2.refs_0_), channel_id=1, source_target_pairs={{0,192},{8,200},{16,208},{24,216},{32,224},{40,232},{48,240},{56,2... | collective-permute-start | bytes 835592 | tf_op jit(solution)/shard_map/ppermute | solution.py:81
  16.0 18.1 %collective-permute-start.3 = (bf16[64,2176]{1,0:T(8,128)(2,1)S(1)}, bf16[64,2176]{1,0:T(8,128)(2,1)S(1)}, u32[]{:S(2)}, u32[]{:S(2)}) collective-permute-start(bf16[64,2176]{1,0:T(8,128)(2,1)S(1)} %pad_maximum_fusion.2.refs_0_), channel_id=1, source_target_pairs={{0,32},{8,40},{16,48},{24,56},{32,64},{40,72},{48,80},{56,88},{64,... | collective-permute-start | bytes 835592 | tf_op jit(solution)/shard_map/ppermute | solution.py:81
  16.8 17.4 %collective-permute-start.4 = (bf16[64,2176]{1,0:T(8,128)(2,1)S(1)}, bf16[64,2176]{1,0:T(8,128)(2,1)S(1)}, u32[]{:S(2)}, u32[]{:S(2)}) collective-permute-start(bf16[64,2176]{1,0:T(8,128)(2,1)S(1)} %pad_maximum_fusion.2.refs_0_), channel_id=1, source_target_pairs={{0,224},{8,232},{16,240},{24,248},{32,0},{40,8},{48,16},{56,24},{6... | collective-permute-start | bytes 835592 | tf_op jit(solution)/shard_map/ppermute | solution.py:81
  23.1 24.5 %collective-permute-start.7 = (bf16[64,2176]{1,0:T(8,128)(2,1)S(1)}, bf16[64,2176]{1,0:T(8,128)(2,1)S(1)}, u32[]{:S(2)}, u32[]{:S(2)}) collective-permute-start(bf16[64,2176]{1,0:T(8,128)(2,1)S(1)} %collective-permute-done.5.refs_3_), channel_id=1, source_target_pairs={{0,32},{8,40},{16,48},{24,56},{32,64},{40,72},{48,80},{56,88},{64,... | collective-permute-start | bytes 835592 | tf_op jit(solution)/shard_map/ppermute | solution.py:81
  29.3 18.4 %collective-permute-start.8 = (bf16[64,2176]{1,0:T(8,128)(2,1)S(1)}, bf16[64,2176]{1,0:T(8,128)(2,1)S(1)}, u32[]{:S(2)}, u32[]{:S(2)}) collective-permute-start(bf16[64,2176]{1,0:T(8,128)(2,1)S(1)} %collective-permute-done.6.refs_4_), channel_id=1, source_target_pairs={{0,224},{8,232},{16,240},{24,248},{32,0},{40,8},{48,16},{56,24},{6... | collective-permute-start | bytes 835592 | tf_op jit(solution)/shard_map/ppermute | solution.py:81
  29.3 18.3 %collective-permute-start.10 = (bf16[32,2176]{1,0:T(8,128)(2,1)S(1)}, bf16[32,2176]{1,0:T(8,128)(2,1)S(1)}, u32[]{:S(2)}, u32[]{:S(2)}) collective-permute-start(bf16[32,2176]{1,0:T(8,128)(2,1)S(1)} %slice.95), channel_id=1, source_target_pairs={{0,192},{8,200},{16,208},{24,216},{32,224},{40,232},{48,240},{56,2... | collective-permute-start | bytes 417800 | tf_op jit(solution)/shard_map/ppermute | solution.py:81
  34.1 13.5 %collective-permute-start.9 = (bf16[32,2176]{1,0:T(8,128)(2,1)S(1)}, bf16[32,2176]{1,0:T(8,128)(2,1)S(1)}, u32[]{:S(2)}, u32[]{:S(2)}) collective-permute-start(bf16[32,2176]{1,0:T(8,128)(2,1)S(1)} %slice.94), channel_id=1, source_target_pairs={{0,64},{8,72},{16,80},{24,88},{32,96},{40,104},{48,112},{56,120},{... | collective-permute-start | bytes 417800 | tf_op jit(solution)/shard_map/ppermute | solution.py:81
  49.8 4.6 %copy-start.2 = (s32[2,512]{1,0:T(2,128)S(1)}, s32[2,512]{1,0:T(2,128)}, u32[]{:S(2)}) copy-start(s32[2,512]{1,0:T(2,128)} %param.7) | copy-start | bytes 12292
  53.3 9.1 %collective-permute-start.19 = (f32[4,128,512]{2,1,0:T(8,128)S(1)}, f32[4,128,512]{2,1,0:T(8,128)}, u32[]{:S(2)}, u32[]{:S(2)}) collective-permute-start(f32[4,128,512]{2,1,0:T(8,128)S(1)} %get-tuple-element.25), channel_id=1, source_target_pairs={{0,1},{1,0},{2,3},{3,2},{4,5},{5,4},{6,7},{7,6},{8,9},{9,8},{10,11... | collective-permute-start | bytes 3145736 | tf_op jit(solution)/shard_map/ppermute | solution.py:362
  55.1 2.1 %collective-permute-start.11 = (f32[4,160,128]{2,1,0:T(8,128)S(1)}, f32[4,160,128]{2,1,0:T(8,128)S(1)}, u32[]{:S(2)}, u32[]{:S(2)}) collective-permute-start(f32[4,160,128]{2,1,0:T(8,128)S(1)} %get-tuple-element.17), channel_id=1, source_target_pairs={{0,1},{1,0},{2,3},{3,2},{4,5},{5,4},{6,7},{7,6},{8,9},{9,8},{10,11... | collective-permute-start | bytes 983048 | tf_op jit(solution)/shard_map/ppermute | solution.py:362
  57.2 7.8 %collective-permute-start.12 = (f32[160,128]{1,0:T(8,128)S(1)}, f32[160,128]{1,0:T(8,128)S(1)}, u32[]{:S(2)}, u32[]{:S(2)}) collective-permute-start(f32[160,128]{1,0:T(8,128)S(1)} %get-tuple-element.33), channel_id=1, source_target_pairs={{0,2},{1,3},{2,4},{3,5},{4,6},{5,7},{6,0},{7,1},{8,10},{9,11},{10,... | collective-permute-start | bytes 245768 | tf_op jit(solution)/shard_map/ppermute | solution.py:363
  58.8 8.2 %collective-permute-start.13 = (f32[160,128]{1,0:T(8,128)S(1)}, f32[160,128]{1,0:T(8,128)S(1)}, u32[]{:S(2)}, u32[]{:S(2)}) collective-permute-start(f32[160,128]{1,0:T(8,128)S(1)} %get-tuple-element.31), channel_id=1, source_target_pairs={{0,4},{1,5},{2,6},{3,7},{4,0},{5,1},{6,2},{7,3},{8,12},{9,13},{10,... | collective-permute-start | bytes 245768 | tf_op jit(solution)/shard_map/ppermute | solution.py:363
  61.4 5.5 %collective-permute-start.14 = (f32[160,128]{1,0:T(8,128)S(1)}, f32[160,128]{1,0:T(8,128)S(1)}, u32[]{:S(2)}, u32[]{:S(2)}) collective-permute-start(f32[160,128]{1,0:T(8,128)S(1)} %get-tuple-element.32), channel_id=1, source_target_pairs={{0,6},{1,7},{2,0},{3,1},{4,2},{5,3},{6,4},{7,5},{8,14},{9,15},{10,... | collective-permute-start | bytes 245768 | tf_op jit(solution)/shard_map/ppermute | solution.py:363
  63.7 9.1 %collective-permute-start.20 = (f32[128,512]{1,0:T(8,128)S(1)}, f32[128,512]{1,0:T(8,128)S(1)}, u32[]{:S(2)}, u32[]{:S(2)}) collective-permute-start(f32[128,512]{1,0:T(8,128)S(1)} %get-tuple-element.30), channel_id=1, source_target_pairs={{0,2},{1,3},{2,4},{3,5},{4,6},{5,7},{6,0},{7,1},{8,10},{9,11},{10,... | collective-permute-start | bytes 786440 | tf_op jit(solution)/shard_map/ppermute | solution.py:363
  64.2 11.9 %collective-permute-start.21 = (f32[128,512]{1,0:T(8,128)S(1)}, f32[128,512]{1,0:T(8,128)S(1)}, u32[]{:S(2)}, u32[]{:S(2)}) collective-permute-start(f32[128,512]{1,0:T(8,128)S(1)} %get-tuple-element.28), channel_id=1, source_target_pairs={{0,4},{1,5},{2,6},{3,7},{4,0},{5,1},{6,2},{7,3},{8,12},{9,13},{10,... | collective-permute-start | bytes 786440 | tf_op jit(solution)/shard_map/ppermute | solution.py:363
  65.0 14.0 %collective-permute-start.22 = (f32[128,512]{1,0:T(8,128)S(1)}, f32[128,512]{1,0:T(8,128)S(1)}, u32[]{:S(2)}, u32[]{:S(2)}) collective-permute-start(f32[128,512]{1,0:T(8,128)S(1)} %get-tuple-element.29), channel_id=1, source_target_pairs={{0,6},{1,7},{2,0},{3,1},{4,2},{5,3},{6,4},{7,5},{8,14},{9,15},{10,... | collective-permute-start | bytes 786440 | tf_op jit(solution)/shard_map/ppermute | solution.py:363
  67.0 17.9 %collective-permute-start.16 = (f32[160,128]{1,0:T(8,128)S(1)}, f32[160,128]{1,0:T(8,128)S(1)}, u32[]{:S(2)}, u32[]{:S(2)}) collective-permute-start(f32[160,128]{1,0:T(8,128)S(1)} %fusion.10.own), channel_id=1, source_target_pairs={{0,4},{1,5},{2,6},{3,7},{4,0},{5,1},{6,2},{7,3},{8,12},{9,13},{10,... | collective-permute-start | bytes 245768 | tf_op jit(solution)/shard_map/ppermute | solution.py:363
  69.2 15.7 %collective-permute-start.17 = (f32[160,128]{1,0:T(8,128)S(1)}, f32[160,128]{1,0:T(8,128)S(1)}, u32[]{:S(2)}, u32[]{:S(2)}) collective-permute-start(f32[160,128]{1,0:T(8,128)S(1)} %fusion.10.own), channel_id=1, source_target_pairs={{0,6},{1,7},{2,0},{3,1},{4,2},{5,3},{6,4},{7,5},{8,14},{9,15},{10,... | collective-permute-start | bytes 245768 | tf_op jit(solution)/shard_map/ppermute | solution.py:363
  72.9 12.1 %collective-permute-start.15 = (f32[160,128]{1,0:T(8,128)S(1)}, f32[160,128]{1,0:T(8,128)S(1)}, u32[]{:S(2)}, u32[]{:S(2)}) collective-permute-start(f32[160,128]{1,0:T(8,128)S(1)} %fusion.10.own), channel_id=1, source_target_pairs={{0,2},{1,3},{2,4},{3,5},{4,6},{5,7},{6,0},{7,1},{8,10},{9,11},{10,... | collective-permute-start | bytes 245768 | tf_op jit(solution)/shard_map/ppermute | solution.py:363
  80.1 9.4 %collective-permute-start.23 = (f32[128,512]{1,0:T(8,128)S(1)}, f32[128,512]{1,0:T(8,128)S(1)}, u32[]{:S(2)}, u32[]{:S(2)}) collective-permute-start(f32[128,512]{1,0:T(8,128)S(1)} %fusion.5), channel_id=1, source_target_pairs={{0,2},{1,3},{2,4},{3,5},{4,6},{5,7},{6,0},{7,1},{8,10},{9,11},{10,... | collective-permute-start | bytes 786440 | tf_op jit(solution)/shard_map/ppermute | solution.py:363
  81.7 12.5 %collective-permute-start.24 = (f32[128,512]{1,0:T(8,128)S(1)}, f32[128,512]{1,0:T(8,128)S(1)}, u32[]{:S(2)}, u32[]{:S(2)}) collective-permute-start(f32[128,512]{1,0:T(8,128)S(1)} %fusion.5), channel_id=1, source_target_pairs={{0,4},{1,5},{2,6},{3,7},{4,0},{5,1},{6,2},{7,3},{8,12},{9,13},{10,... | collective-permute-start | bytes 786440 | tf_op jit(solution)/shard_map/ppermute | solution.py:363
  84.9 10.4 %collective-permute-start.25 = (f32[128,512]{1,0:T(8,128)S(1)}, f32[128,512]{1,0:T(8,128)S(1)}, u32[]{:S(2)}, u32[]{:S(2)}) collective-permute-start(f32[128,512]{1,0:T(8,128)S(1)} %fusion.5), channel_id=1, source_target_pairs={{0,6},{1,7},{2,0},{3,1},{4,2},{5,3},{6,4},{7,5},{8,14},{9,15},{10,... | collective-permute-start | bytes 786440 | tf_op jit(solution)/shard_map/ppermute | solution.py:363
  85.0 13.2 %collective-permute-start.18 = (f32[4,160,128]{2,1,0:T(8,128)S(1)}, f32[4,160,128]{2,1,0:T(8,128)S(1)}, u32[]{:S(2)}, u32[]{:S(2)}) collective-permute-start(f32[4,160,128]{2,1,0:T(8,128)S(1)} %pad_maximum_fusion.1), channel_id=1, source_target_pairs={{0,1},{1,0},{2,3},{3,2},{4,5},{5,4},{6,7},{7,6},{8,9},{9,8},{10,11... | collective-permute-start | bytes 983048 | tf_op jit(solution)/shard_map/ppermute | solution.py:362
  95.3 25.1 %collective-permute-start.26 = (f32[4,128,512]{2,1,0:T(8,128)S(1)}, f32[4,128,512]{2,1,0:T(8,128)S(1)}, u32[]{:S(2)}, u32[]{:S(2)}) collective-permute-start(f32[4,128,512]{2,1,0:T(8,128)S(1)} %pad_maximum_fusion.near), channel_id=1, source_target_pairs={{0,1},{1,0},{2,3},{3,2},{4,5},{5,4},{6,7},{7,6},{8,9},{9,8},{10,11... | collective-permute-start | bytes 3145736 | tf_op jit(solution)/shard_map/ppermute | solution.py:362
  109.1 11.4 %copy-start = (bf16[1024,64]{0,1:T(8,128)(2,1)S(1)}, bf16[1024,64]{0,1:T(8,128)(2,1)}, u32[]{:S(2)}) copy-start(bf16[1024,64]{0,1:T(8,128)(2,1)} %param.10) | copy-start | bytes 393220
where the time goes:
time: 122 us
  starting transfers between devices  45.3 us (37%)
  waiting for transfers between devices  41.3 us (34%)
  Pallas kernels  29.7 us (24%)
  other arithmetic  4.18 us (3%)
    ppermute x8, waiting for transfers between devices, tower(): hop = lambda a, k: lax.ppermute(a, 'row', shift_z(k))  21.9 us
    ppermute x8, starting transfers between devices, tower(): hop = lambda a, k: lax.ppermute(a, 'row', shift_z(k))  16.1 us
    ppermute x12, starting transfers between devices, shards(): along = lambda a, k: lax.ppermute(a, 'layer', shift_y(k))  15.9 us
    ppermute x12, waiting for transfers between devices, shards(): along = lambda a, k: lax.ppermute(a, 'layer', shift_y(k))  15.8 us
    pallas_call x1, Pallas kernels, weigh(): pl.pallas_call(weights_kernel, name='weigh', out_shape=(square, square, j...  11.3 us
    pallas_call x1, Pallas kernels, factor(): pl.pallas_call(factor_kernel, name='factor', out_shape=(square, square),...  10.9 us
    ppermute x4, starting transfers between devices, shards(): swap = lambda a: lax.ppermute(a, 'layer', SWAP)  7.64 us
    ppermute x3, starting transfers between devices, shards(): near = [held] + [lax.ppermute(held, 'row', shift_x(k)) for k in (1, 2, 3)]  5.66 us
  transfers between devices with their start and end apart: 27, of which 14 were waited for; matrix products, arithmetic and copies ran while one was open for 3% of the time, Pallas kernels for 18%

commit v1 on v0

--- a/solution.py
+++ b/solution.py
@@ -35,6 +35,7 @@
     return [(y * NC + c, (y + k) % NY * NC + c) for y in range(NY) for c in range(NC)]
 
 
+PAIRS = [[(y * NC + c, (y ^ 1 if n == 0 else NY - 1 - y) * NC + c) for y in range(NY) for c in range(NC)] for n in range(2)]
 SWAP = [(y * NC + c, y * NC + 1 - c) for y in range(NY) for c in range(NC)]
 
 
@@ -87,7 +88,7 @@
 
 def gram_kernel(*refs):
     pieces, (rows, sides, other, mine, blocks) = refs[:9], refs[9:]
-    z, x, y, c = place()
+    z, x, _, c = place()
     for piece, (turn, first) in zip(pieces, PIECES):
 
         @pl.loop(0, piece.shape[0] // 16)
@@ -106,15 +107,15 @@
         for j in range(i + 1):
             blocks[at] = part[:, 128 * j : 128 * j + 128]
             at += 1
-    for k in range(NY):
+    for n in range(2):
         for out, core in ((other, 1 - c), (mine, c)):
-            first = pl.multiple_of(64 * core + 16 * lax.rem(y + k, NY), 16)
+            first = pl.multiple_of(64 * core + 32 * n, 32)
             for b in range(len(BLOCKS)):
-                out[k, 16 * b : 16 * b + 16] = blocks[b, pl.ds(first, 16), :]
+                out[n, 32 * b : 32 * b + 32] = blocks[b, pl.ds(first, 32), :]
 
 
 def gram(pieces):
-    chunk = jax.ShapeDtypeStruct((NY, 16 * len(BLOCKS), 128), F32)
+    chunk = jax.ShapeDtypeStruct((2, 32 * len(BLOCKS), 128), F32)
     return pl.pallas_call(
         gram_kernel,
         name="gram",
@@ -197,38 +198,39 @@
     for p in range(8):
         more = p + 1 < 8
         if more:
-            below = [lanes(a[p + 1], 8 * p + 8 + c) for c in range(8)]
-            right = [lanes(a[p], 8 * p + 8 + c) for c in range(8)]
-        old = {(c, g): lanes(a[g], 8 * p + c) for g in range(p + 1, 8) for c in range(8)}
+            below = [lanes(a[p + 1], 8 * p + c) for c in range(8)]
+            coming = [lanes(a[p + 1], 8 * p + 8 + c) for c in range(8)]
+        old = {(c, g): lanes(a[g], 8 * p + c) for g in range(p + 2, 8) for c in range(8)}
         factor_rows = solved_rows = a[p]
-        pivots = jnp.ones((8, 128), F32)
-        scale = pivots
+        pivots = scale = jnp.ones((8, 128), F32)
         for j in range(8):
             d = spread(column[j], j)
             r = 1.0 / d
             full = jnp.where(row != j, column[j], 0.0)
-            low = jnp.where(row > j, column[j], 0.0)
-            full_r = full * r
-            lead = spread(factor_rows, j) * r
-            for c in range(j + 1, 8):
-                if c == j + 1:
-                    column[c] = column[c] - (full * spread(column[c], j)) * r
-                else:
-                    column[c] = column[c] - full_r * spread(column[c], j)
-            if more:
-                right = [v - full_r * spread(v, j) for v in right]
-            solved_rows = solved_rows - full * lead
-            factor_rows = factor_rows - low * lead
+            lead = spread(solved_rows, j)
+            if j > 0:
+                factor_rows = jnp.where(row == j, lead, factor_rows)
             pivots = jnp.where(row == j, d, pivots)
             scale = jnp.where(row == j, r, scale)
+            heads = {c: spread(column[c], j) for c in range(j + 1, 8)}
+            heads_r = {c: v * r for c, v in heads.items()}
+            for c in range(j + 1, 8):
+                column[c] = column[c] - ((full * heads[c]) * r if c == j + 1 else full * heads_r[c])
+            solved_rows = solved_rows - full * (lead * r)
+            if more:
+                below_r = below[j] * r
+                coming = [v - below_r * spread(below[j], c) for c, v in enumerate(coming)]
+                a[p + 1] = a[p + 1] - below_r * lead
+                for c in range(j + 1, 8):
+                    below[c] = below[c] - below[j] * heads_r[c]
         done.append(factor_rows * lax.rsqrt(pivots))
         if more:
-            right = [v * scale for v in right]
-            column = [below[c] - tree_sum(old[k, p + 1] * spread(right[c], k) for k in range(8)) for c in range(8)]
-        solved_rows = solved_rows * scale
-        heads = [spread(solved_rows, c) for c in range(8)]
-        for g in range(p + 1, 8):
-            a[g] = a[g] - tree_sum(old[c, g] * heads[c] for c in range(8))
+            column = coming
+        if p + 2 < 8:
+            solved_rows = solved_rows * scale
+            leads = [spread(solved_rows, c) for c in range(8)]
+            for g in range(p + 2, 8):
+                a[g] = a[g] - tree_sum(old[c, g] * leads[c] for c in range(8))
     return jnp.concatenate(done, axis=0)[:, STEP:]
 
 
@@ -281,16 +283,14 @@
 STEPS_SCRATCH = [pltpu.VMEM((STEP, STEP), F32)] * 3
 
 
-def factor_kernel(cov, own, near1, near2, near3, far, a, e, block, half, cross):
-    _, _, y, c = place()
-    for k in range(NY):
-        for core in range(NC):
-            piece = (own, near1, near2, near3)[k] if core == 0 else far.at[k]
-            which = c if core == 0 else 1 - c
-            first = pl.multiple_of(64 * which + 16 * lax.rem(y - k + NY, NY), 16)
+def factor_kernel(cov, near, far, a, e, block, half, cross):
+    _, _, _, c = place()
+    for n in range(2):
+        for piece, core in ((near, c), (far, 1 - c)):
+            first = pl.multiple_of(64 * core + 32 * n, 32)
             for b, (i, j) in enumerate(BLOCKS):
-                at = (pl.ds(128 * i + first, 16), slice(128 * j, 128 * j + 128))
-                a[at] = cov[at] - piece[16 * b : 16 * b + 16]
+                at = (pl.ds(128 * i + first, 32), slice(128 * j, 128 * j + 128))
+                a[at] = cov[at] - piece[n, 32 * b : 32 * b + 32]
     e[...] = jnp.zeros_like(e)
     block[...] = a[:STEP, :STEP]
     factor_steps(a, e, block, half, cross, 0)
@@ -302,7 +302,7 @@
         factor_kernel,
         name="factor",
         out_shape=(square, square),
-        in_specs=[VMEM] * 6,
+        in_specs=[VMEM] * 3,
         out_specs=(VMEM, VMEM),
         scratch_shapes=STEPS_SCRATCH,
         compiler_params=grant(10),
@@ -367,17 +367,17 @@
     pieces = tower(jnp.concatenate(near, axis=0))
     rows, sides, gram_other, gram_mine = gram(pieces)
     gram_far = swap(gram_other)
-    gram_sum = [gram_mine[k] + gram_far[k] for k in range(NY)]
-    gram_in = [along(gram_sum[k], k) for k in (1, 2, 3)]
-    gram_own = gram_sum[0] + (gram_in[0] + gram_in[1] + gram_in[2])
-    gram_near = [gram_own] + [along(gram_own, k) for k in (1, 2, 3)]
-    gram_far = swap(jnp.stack(gram_near))
+    sums = [gram_mine[n] + gram_far[n] for n in range(2)]
+    sums = [sums[n] + lax.ppermute(sums[n], "layer", PAIRS[n]) for n in range(2)]
+    sums = [sums[n] + lax.ppermute(sums[n], "layer", PAIRS[1 - n]) for n in range(2)]
+    gram_near = jnp.stack(sums)
+    gram_far = swap(gram_near)
 
     points = lax.dynamic_slice_in_dim(window_points, 512 * c + 128 * y, 128, 1)
     cov = matern(pivot_points, pivot_points) + nugget_value * jnp.eye(COUNT, dtype=F32)
     covered = matern(points, pivot_points)
     cov, covered = lax.optimization_barrier((cov, covered))
-    a, e = factor(cov, *gram_near, gram_far)
+    a, e = factor(cov, gram_near, gram_far)
     weights = weigh(a, e, sides)
 
     schur_other, schur_mine = schur(window_factor, rows)

time: 122 us -> 121 us (level)
  waiting for transfers between devices: 41.3 us -> 47 us
  starting transfers between devices: 45.3 us -> 41.6 us
  Pallas kernels: 29.7 us -> 28 us
  other arithmetic: 4.18 us -> 2.87 us
    ppermute x12 -> x6, starting transfers between devices: 15.9 us -> 7.62 us  [shards(): along = lambda a, k: lax.ppermute(a, 'layer', shift_y(k))]
    ppermute x0 -> x4, starting transfers between devices: none -> 6.2 us  [the longest x2 3.29 us: shards(): lax.ppermute(sums[n], 'layer', PAIRS[n])]
    ppermute x12 -> x6, waiting for transfers between devices: 15.8 us -> 20.2 us  [shards(): along = lambda a, k: lax.ppermute(a, 'layer', shift_y(k))]
    ppermute x0 -> x4, waiting for transfers between devices: none -> 1.96 us  [the longest x2 1.95 us: shards(): lax.ppermute(sums[n], 'layer', PAIRS[n])]
    ppermute x4, starting transfers between devices: 7.64 us -> 6.02 us  [shards(): swap = lambda a: lax.ppermute(a, 'layer', SWAP)]
  transfers between devices with their start and end apart: 27 -> 25, of which waited for: 14 -> 14; matrix products, arithmetic and copies ran while one was open for 3% -> 2% of each run, Pallas kernels for 18% -> 17%
where the time goes in v1:
time: 121 us
  waiting for transfers between devices  47 us (39%)
  starting transfers between devices  41.6 us (34%)
  Pallas kernels  28 us (23%)
  other arithmetic  2.87 us (2%)
    ppermute x8, waiting for transfers between devices, tower(): hop = lambda a, k: lax.ppermute(a, 'row', shift_z(k))  21.2 us
    ppermute x6, waiting for transfers between devices, shards(): along = lambda a, k: lax.ppermute(a, 'layer', shift_y(k))  20.2 us
    ppermute x8, starting transfers between devices, tower(): hop = lambda a, k: lax.ppermute(a, 'row', shift_z(k))  16.1 us
    pallas_call x1, Pallas kernels, weigh(): pl.pallas_call(weights_kernel, name='weigh', out_shape=(square, square, j...  10.4 us
    pallas_call x1, Pallas kernels, factor(): pl.pallas_call(factor_kernel, name='factor', out_shape=(square, square),...  10 us
    ppermute x6, starting transfers between devices, shards(): along = lambda a, k: lax.ppermute(a, 'layer', shift_y(k))  7.62 us
    ppermute x4, starting transfers between devices, shards(): swap = lambda a: lax.ppermute(a, 'layer', SWAP)  6.02 us
    ppermute x3, starting transfers between devices, shards(): near = [held] + [lax.ppermute(held, 'row', shift_x(k)) for k in (1, 2, 3)]  5.64 us
  transfers between devices with their start and end apart: 25, of which 14 were waited for; matrix products, arithmetic and copies ran while one was open for 2% of the time, Pallas kernels for 17%

profile of v1, /device:TPU:1, one launch (start us, length us, event | category | flops | bytes accessed | tf_op | source)
XLA Modules:
  0.0 121.2 jit_solution(3980607576400581618)
XLA Ops:
  0.6 0.9 concatenate.6
  1.6 2.0 %collective-permute-start = (bf16[16,2176]{1,0:T(8,128)(2,1)S(1)}, bf16[16,2176]{1,0:T(8,128)(2,1)S(1)}, u32[]{:S(2)}, u32[]{:S(2)}) collective-permute-start(bf16[16,2176]{1,0:T(8,128)(2,1)S(1)} %concatenate.6), channel_id=1, source_target_pairs={{0,8},{8,16},{16,24},{24,0},{32,40},{40,48},{48,56},{56,32},{64,72... | collective-permute-start | bytes 208904 | tf_op jit(solution)/shard_map/ppermute | solution.py:366
  3.6 2.5 %collective-permute-start.1 = (bf16[16,2176]{1,0:T(8,128)(2,1)S(1)}, bf16[16,2176]{1,0:T(8,128)(2,1)S(1)}, u32[]{:S(2)}, u32[]{:S(2)}) collective-permute-start(bf16[16,2176]{1,0:T(8,128)(2,1)S(1)} %concatenate.6), channel_id=1, source_target_pairs={{0,16},{8,24},{16,0},{24,8},{32,48},{40,56},{48,32},{56,40},{64,80... | collective-permute-start | bytes 208904 | tf_op jit(solution)/shard_map/ppermute | solution.py:366
  6.1 1.2 collective-permute-start.2
  7.2 0.0 collective-permute-done
  7.2 1.6 %collective-permute-done.1 = bf16[16,2176]{1,0:T(8,128)(2,1)S(1)} collective-permute-done((bf16[16,2176]{1,0:T(8,128)(2,1)S(1)}, bf16[16,2176]{1,0:T(8,128)(2,1)S(1)}, u32[]{:S(2)}, u32[]{:S(2)}) %collective-permute-start.1) | collective-permute-done | bytes 69664 | tf_op jit(solution)/shard_map/ppermute | solution.py:366
  8.9 0.7 collective-permute-done.2
  9.5 3.4 %collective-permute-start.5 = (bf16[64,2176]{1,0:T(8,128)(2,1)S(1)}, bf16[64,2176]{1,0:T(8,128)(2,1)S(1)}, u32[]{:S(2)}, u32[]{:S(2)}) collective-permute-start(bf16[64,2176]{1,0:T(8,128)(2,1)S(1)} %pad_maximum_fusion.2.refs_0_), channel_id=1, source_target_pairs={{0,64},{8,72},{16,80},{24,88},{32,96},{40,104},{48,112},{56,120},{... | collective-permute-start | bytes 835592 | tf_op jit(solution)/shard_map/ppermute | solution.py:82
  12.9 3.1 %collective-permute-start.6 = (bf16[64,2176]{1,0:T(8,128)(2,1)S(1)}, bf16[64,2176]{1,0:T(8,128)(2,1)S(1)}, u32[]{:S(2)}, u32[]{:S(2)}) collective-permute-start(bf16[64,2176]{1,0:T(8,128)(2,1)S(1)} %pad_maximum_fusion.2.refs_0_), channel_id=1, source_target_pairs={{0,192},{8,200},{16,208},{24,216},{32,224},{40,232},{48,240},{56,2... | collective-permute-start | bytes 835592 | tf_op jit(solution)/shard_map/ppermute | solution.py:82
  16.0 0.7 collective-permute-start.3
  16.8 1.9 %collective-permute-start.4 = (bf16[64,2176]{1,0:T(8,128)(2,1)S(1)}, bf16[64,2176]{1,0:T(8,128)(2,1)S(1)}, u32[]{:S(2)}, u32[]{:S(2)}) collective-permute-start(bf16[64,2176]{1,0:T(8,128)(2,1)S(1)} %pad_maximum_fusion.2.refs_0_), channel_id=1, source_target_pairs={{0,224},{8,232},{16,240},{24,248},{32,0},{40,8},{48,16},{56,24},{6... | collective-permute-start | bytes 835592 | tf_op jit(solution)/shard_map/ppermute | solution.py:82
  18.7 4.3 %collective-permute-done.5.refs_3_ = bf16[64,2176]{1,0:T(8,128)(2,1)S(1)} collective-permute-done((bf16[64,2176]{1,0:T(8,128)(2,1)S(1)}, bf16[64,2176]{1,0:T(8,128)(2,1)S(1)}, u32[]{:S(2)}, u32[]{:S(2)}) %collective-permute-start.5) | collective-permute-done | bytes 278560 | tf_op jit(solution)/shard_map/ppermute | solution.py:82
  23.0 5.4 %collective-permute-start.7 = (bf16[64,2176]{1,0:T(8,128)(2,1)S(1)}, bf16[64,2176]{1,0:T(8,128)(2,1)S(1)}, u32[]{:S(2)}, u32[]{:S(2)}) collective-permute-start(bf16[64,2176]{1,0:T(8,128)(2,1)S(1)} %collective-permute-done.5.refs_3_), channel_id=1, source_target_pairs={{0,32},{8,40},{16,48},{24,56},{32,64},{40,72},{48,80},{56,88},{64,... | collective-permute-start | bytes 835592 | tf_op jit(solution)/shard_map/ppermute | solution.py:82
  28.4 0.8 collective-permute-done.6.refs_4_
  29.2 0.0 collective-permute-start.8
  29.2 0.7 convert_element_type.4
  29.9 1.5 %collective-permute-start.10 = (bf16[32,2176]{1,0:T(8,128)(2,1)S(1)}, bf16[32,2176]{1,0:T(8,128)(2,1)S(1)}, u32[]{:S(2)}, u32[]{:S(2)}) collective-permute-start(bf16[32,2176]{1,0:T(8,128)(2,1)S(1)} %slice.79), channel_id=1, source_target_pairs={{0,192},{8,200},{16,208},{24,216},{32,224},{40,232},{48,240},{56,2... | collective-permute-start | bytes 417800 | tf_op jit(solution)/shard_map/ppermute | solution.py:82
  31.5 2.6 %collective-permute-done.3.refs_1_ = bf16[64,2176]{1,0:T(8,128)(2,1)S(1)} collective-permute-done((bf16[64,2176]{1,0:T(8,128)(2,1)S(1)}, bf16[64,2176]{1,0:T(8,128)(2,1)S(1)}, u32[]{:S(2)}, u32[]{:S(2)}) %collective-permute-start.3) | collective-permute-done | bytes 278560 | tf_op jit(solution)/shard_map/ppermute | solution.py:82
  34.1 0.0 collective-permute-start.9
  34.1 0.1 collective-permute-done.4.refs_2_
  34.2 13.4 %collective-permute-done.10.refs_8_ = bf16[32,2176]{1,0:T(8,128)(2,1)S(1)} collective-permute-done((bf16[32,2176]{1,0:T(8,128)(2,1)S(1)}, bf16[32,2176]{1,0:T(8,128)(2,1)S(1)}, u32[]{:S(2)}, u32[]{:S(2)}) %collective-permute-start.10) | collective-permute-done | bytes 139296 | tf_op jit(solution)/shard_map/ppermute | solution.py:82
  47.6 0.0 collective-permute-done.9.refs_7_
  47.6 0.0 collective-permute-done.7.refs_5_
  47.6 0.0 collective-permute-done.8.refs_6_
  47.6 2.3 %gram.1 = (bf16[512,2048]{1,0:T(8,128)(2,1)S(1)}, bf16[512,128]{1,0:T(8,128)(2,1)S(1)}, f32[2,320,128]{2,1,0:T(8,128)S(1)}, f32[2,320,128]{2,1,0:T(8,128)S(1)}) custom-call(bf16[64,2176]{1,0:T(8,128)(2,1)S(1)} %pad_maximum_fusion.2.refs_0_, bf16[64,2176]{1,0:T(8,128)(2,1)S(1)} %collective-permute-done.3.refs_1_, ...), custom_call_target="tpu_custom_call" | custom-call | flops 1073741824 | bytes 2097152 | tf_op jit(solution)/shard_map/gram/pallas_call | solution.py:119
  49.9 3.5 %schur.1 = (f32[4,128,512]{2,1,0:T(8,128)S(1)}, f32[4,128,512]{2,1,0:T(8,128)S(1)}) custom-call(bf16[1024,2048]{1,0:T(8,128)(2,1)S(1)} %copy-done.1, bf16[512,2048]{1,0:T(8,128)(2,1)S(1)} %get-tuple-element.23.rows), custom_call_target="tpu_custom_call" | custom-call | flops 2147483648 | bytes 8388608 | tf_op jit(solution)/shard_map/schur/pallas_call | solution.py:169
  53.4 1.1 collective-permute-start.17
  54.5 0.7 dynamic-slice_convert_fusion
  55.1 0.0 collective-permute-start.11
  55.2 0.7 select_add_fusion.cov
  55.9 1.3 %collective-permute-done.11 = f32[2,320,128]{2,1,0:T(8,128)S(1)} collective-permute-done((f32[2,320,128]{2,1,0:T(8,128)S(1)}, f32[2,320,128]{2,1,0:T(8,128)S(1)}, u32[]{:S(2)}, u32[]{:S(2)}) %collective-permute-start.11) | collective-permute-done | bytes 327712 | tf_op jit(solution)/shard_map/ppermute | solution.py:362
  57.3 1.4 %collective-permute-start.12 = (f32[320,128]{1,0:T(8,128)S(1)}, f32[320,128]{1,0:T(8,128)S(1)}, u32[]{:S(2)}, u32[]{:S(2)}) collective-permute-start(f32[320,128]{1,0:T(8,128)S(1)} %get-tuple-element.31), channel_id=1, source_target_pairs={{0,2},{1,3},{2,0},{3,1},{4,6},{5,7},{6,4},{7,5},{8,10},{9,11},{10,... | collective-permute-start | bytes 491528 | tf_op jit(solution)/shard_map/ppermute | solution.py:371
  58.6 1.9 %collective-permute-start.14 = (f32[320,128]{1,0:T(8,128)S(1)}, f32[320,128]{1,0:T(8,128)S(1)}, u32[]{:S(2)}, u32[]{:S(2)}) collective-permute-start(f32[320,128]{1,0:T(8,128)S(1)} %get-tuple-element.32), channel_id=1, source_target_pairs={{0,6},{1,7},{2,4},{3,5},{4,2},{5,3},{6,0},{7,1},{8,14},{9,15},{10,... | collective-permute-start | bytes 491528 | tf_op jit(solution)/shard_map/ppermute | solution.py:371
  60.5 0.2 exponential_multiply_fusion
  60.8 1.9 %collective-permute-done.12 = f32[320,128]{1,0:T(8,128)S(1)} collective-permute-done((f32[320,128]{1,0:T(8,128)S(1)}, f32[320,128]{1,0:T(8,128)S(1)}, u32[]{:S(2)}, u32[]{:S(2)}) %collective-permute-start.12) | collective-permute-done | bytes 163872 | tf_op jit(solution)/shard_map/ppermute | solution.py:371
  62.7 2.8 %collective-permute-start.13 = (f32[320,128]{1,0:T(8,128)S(1)}, f32[320,128]{1,0:T(8,128)S(1)}, u32[]{:S(2)}, u32[]{:S(2)}) collective-permute-start(f32[320,128]{1,0:T(8,128)S(1)} %add.96), channel_id=1, source_target_pairs={{0,6},{1,7},{2,4},{3,5},{4,2},{5,3},{6,0},{7,1},{8,14},{9,15},{10,... | collective-permute-start | bytes 491528 | tf_op jit(solution)/shard_map/ppermute | solution.py:372
  65.6 0.0 collective-permute-done.14
  65.6 0.1 collective-permute-start.15
  65.7 0.0 collective-permute-done.17
  65.7 0.1 fusion.1
  65.9 1.5 %collective-permute-start.18 = (f32[128,512]{1,0:T(8,128)S(1)}, f32[128,512]{1,0:T(8,128)S(1)}, u32[]{:S(2)}, u32[]{:S(2)}) collective-permute-start(f32[128,512]{1,0:T(8,128)S(1)} %get-tuple-element.30), channel_id=1, source_target_pairs={{0,2},{1,3},{2,4},{3,5},{4,6},{5,7},{6,0},{7,1},{8,10},{9,11},{10,... | collective-permute-start | bytes 786440 | tf_op jit(solution)/shard_map/ppermute | solution.py:363
  67.4 1.1 collective-permute-start.19
  68.5 2.0 %collective-permute-start.20 = (f32[128,512]{1,0:T(8,128)S(1)}, f32[128,512]{1,0:T(8,128)S(1)}, u32[]{:S(2)}, u32[]{:S(2)}) collective-permute-start(f32[128,512]{1,0:T(8,128)S(1)} %get-tuple-element.29), channel_id=1, source_target_pairs={{0,6},{1,7},{2,0},{3,1},{4,2},{5,3},{6,4},{7,5},{8,14},{9,15},{10,... | collective-permute-start | bytes 786440 | tf_op jit(solution)/shard_map/ppermute | solution.py:363
  70.4 0.0 collective-permute-done.13
  70.5 0.0 collective-permute-done.15
  70.5 3.8 %collective-permute-done.18 = f32[128,512]{1,0:T(8,128)S(1)} collective-permute-done((f32[128,512]{1,0:T(8,128)S(1)}, f32[128,512]{1,0:T(8,128)S(1)}, u32[]{:S(2)}, u32[]{:S(2)}) %collective-permute-start.18) | collective-permute-done | bytes 262176 | tf_op jit(solution)/shard_map/ppermute | solution.py:363
  74.3 7.8 %collective-permute-done.19 = f32[128,512]{1,0:T(8,128)S(1)} collective-permute-done((f32[128,512]{1,0:T(8,128)S(1)}, f32[128,512]{1,0:T(8,128)S(1)}, u32[]{:S(2)}, u32[]{:S(2)}) %collective-permute-start.19) | collective-permute-done | bytes 262176 | tf_op jit(solution)/shard_map/ppermute | solution.py:363
  82.2 0.0 collective-permute-done.20
  82.2 0.2 fusion.5
  82.3 0.5 collective-permute-start.21
  82.9 2.4 %collective-permute-start.22 = (f32[128,512]{1,0:T(8,128)S(1)}, f32[128,512]{1,0:T(8,128)S(1)}, u32[]{:S(2)}, u32[]{:S(2)}) collective-permute-start(f32[128,512]{1,0:T(8,128)S(1)} %fusion.5), channel_id=1, source_target_pairs={{0,4},{1,5},{2,6},{3,7},{4,0},{5,1},{6,2},{7,3},{8,12},{9,13},{10,... | collective-permute-start | bytes 786440 | tf_op jit(solution)/shard_map/ppermute | solution.py:363
  85.2 0.1 collective-permute-start.23
  85.4 2.9 %collective-permute-start.16 = (f32[2,320,128]{2,1,0:T(8,128)S(1)}, f32[2,320,128]{2,1,0:T(8,128)S(1)}, u32[]{:S(2)}, u32[]{:S(2)}) collective-permute-start(f32[2,320,128]{2,1,0:T(8,128)S(1)} %pad_maximum_fusion.1.near), channel_id=1, source_target_pairs={{0,1},{1,0},{2,3},{3,2},{4,5},{5,4},{6,7},{7,6},{8,9},{9,8},{10,11... | collective-permute-start | bytes 983048 | tf_op jit(solution)/shard_map/ppermute | solution.py:362
  88.3 0.5 collective-permute-done.21
  88.8 7.0 %collective-permute-done.22 = f32[128,512]{1,0:T(8,128)S(1)} collective-permute-done((f32[128,512]{1,0:T(8,128)S(1)}, f32[128,512]{1,0:T(8,128)S(1)}, u32[]{:S(2)}, u32[]{:S(2)}) %collective-permute-start.22) | collective-permute-done | bytes 262176 | tf_op jit(solution)/shard_map/ppermute | solution.py:363
  95.8 1.1 collective-permute-done.23
  96.9 0.1 pad_maximum_fusion.near
  97.0 2.0 %collective-permute-start.24 = (f32[4,128,512]{2,1,0:T(8,128)S(1)}, f32[4,128,512]{2,1,0:T(8,128)S(1)}, u32[]{:S(2)}, u32[]{:S(2)}) collective-permute-start(f32[4,128,512]{2,1,0:T(8,128)S(1)} %pad_maximum_fusion.near), channel_id=1, source_target_pairs={{0,1},{1,0},{2,3},{3,2},{4,5},{5,4},{6,7},{7,6},{8,9},{9,8},{10,11... | collective-permute-start | bytes 3145736 | tf_op jit(solution)/shard_map/ppermute | solution.py:362
  98.9 0.0 collective-permute-done.16.far
  99.0 10.0 %factor.1 = (f32[512,512]{1,0:T(8,128)S(1)}, f32[512,512]{1,0:T(8,128)S(1)}) custom-call(f32[512,512]{1,0:T(8,128)S(1)} %select_add_fusion.cov, f32[2,320,128]{2,1,0:T(8,128)S(1)} %pad_maximum_fusion.1.near, f32[2,320,128]{2,1,0:T(8,128)S(1)} %collective-permute-done.16.far), custom_call_target="tpu_custom_call" | custom-call | flops 10000000000 | bytes 4194304 | tf_op jit(solution)/shard_map/factor/pallas_call | solution.py:301
  109.0 0.0 copy-start
  109.0 10.4 %weigh.1 = (f32[512,512]{1,0:T(8,128)S(1)}, f32[512,512]{1,0:T(8,128)S(1)}, f32[128,512]{1,0:T(8,128)S(1)}) custom-call(f32[512,512]{1,0:T(8,128)S(1)} %get-tuple-element.18.a_in, f32[512,512]{1,0:T(8,128)S(1)} %get-tuple-element.19.e_in, bf16[512,128]{1,0:T(8,128)(2,1)S(1)} %get-tuple-element.20.sides), custom_call_target="tpu_custom_call", output_to_operand_aliasing={{0}: (0, {}), {1}: (1, {})} | custom-call | flops 10000000000 | bytes 4194304 | tf_op jit(solution)/shard_map/weigh/pallas_call | solution.py:324
  119.5 0.0 collective-permute-done.24.far
  119.5 1.8 %finish.1 = (f32[64,1024]{1,0:T(8,128)}, f32[64,1024]{1,0:T(8,128)}) custom-call(f32[128,512]{1,0:T(8,128)S(1)} %get-tuple-element.21.weights, f32[4,128,512]{2,1,0:T(8,128)S(1)} %pad_maximum_fusion.near, f32[4,128,512]{2,1,0:T(8,128)S(1)} %collective-permute-done.24.far, bf16[64,1024]{1,0:T(8,128)(2,1)S(1)} %bitcast.33), custom_call_target="tpu_custom_call" | custom-call | flops 402653184 | bytes 3145728 | tf_op jit(solution)/shard_map/finish/pallas_call | solution.py:349
  (15 shorter events, 0.2 us)
Async XLA Ops:
  1.6 5.6 %collective-permute-start = (bf16[16,2176]{1,0:T(8,128)(2,1)S(1)}, bf16[16,2176]{1,0:T(8,128)(2,1)S(1)}, u32[]{:S(2)}, u32[]{:S(2)}) collective-permute-start(bf16[16,2176]{1,0:T(8,128)(2,1)S(1)} %concatenate.6), channel_id=1, source_target_pairs={{0,8},{8,16},{16,24},{24,0},{32,40},{40,48},{48,56},{56,32},{64,72... | collective-permute-start | bytes 208904 | tf_op jit(solution)/shard_map/ppermute | solution.py:366
  3.6 5.2 %collective-permute-start.1 = (bf16[16,2176]{1,0:T(8,128)(2,1)S(1)}, bf16[16,2176]{1,0:T(8,128)(2,1)S(1)}, u32[]{:S(2)}, u32[]{:S(2)}) collective-permute-start(bf16[16,2176]{1,0:T(8,128)(2,1)S(1)} %concatenate.6), channel_id=1, source_target_pairs={{0,16},{8,24},{16,0},{24,8},{32,48},{40,56},{48,32},{56,40},{64,80... | collective-permute-start | bytes 208904 | tf_op jit(solution)/shard_map/ppermute | solution.py:366
  6.1 3.5 %collective-permute-start.2 = (bf16[16,2176]{1,0:T(8,128)(2,1)S(1)}, bf16[16,2176]{1,0:T(8,128)(2,1)S(1)}, u32[]{:S(2)}, u32[]{:S(2)}) collective-permute-start(bf16[16,2176]{1,0:T(8,128)(2,1)S(1)} %concatenate.6), channel_id=1, source_target_pairs={{0,24},{8,0},{16,8},{24,16},{32,56},{40,32},{48,40},{56,48},{64,88... | collective-permute-start | bytes 208904 | tf_op jit(solution)/shard_map/ppermute | solution.py:366
  9.5 13.5 %collective-permute-start.5 = (bf16[64,2176]{1,0:T(8,128)(2,1)S(1)}, bf16[64,2176]{1,0:T(8,128)(2,1)S(1)}, u32[]{:S(2)}, u32[]{:S(2)}) collective-permute-start(bf16[64,2176]{1,0:T(8,128)(2,1)S(1)} %pad_maximum_fusion.2.refs_0_), channel_id=1, source_target_pairs={{0,64},{8,72},{16,80},{24,88},{32,96},{40,104},{48,112},{56,120},{... | collective-permute-start | bytes 835592 | tf_op jit(solution)/shard_map/ppermute | solution.py:82
  12.9 16.3 %collective-permute-start.6 = (bf16[64,2176]{1,0:T(8,128)(2,1)S(1)}, bf16[64,2176]{1,0:T(8,128)(2,1)S(1)}, u32[]{:S(2)}, u32[]{:S(2)}) collective-permute-start(bf16[64,2176]{1,0:T(8,128)(2,1)S(1)} %pad_maximum_fusion.2.refs_0_), channel_id=1, source_target_pairs={{0,192},{8,200},{16,208},{24,216},{32,224},{40,232},{48,240},{56,2... | collective-permute-start | bytes 835592 | tf_op jit(solution)/shard_map/ppermute | solution.py:82
  16.0 18.1 %collective-permute-start.3 = (bf16[64,2176]{1,0:T(8,128)(2,1)S(1)}, bf16[64,2176]{1,0:T(8,128)(2,1)S(1)}, u32[]{:S(2)}, u32[]{:S(2)}) collective-permute-start(bf16[64,2176]{1,0:T(8,128)(2,1)S(1)} %pad_maximum_fusion.2.refs_0_), channel_id=1, source_target_pairs={{0,32},{8,40},{16,48},{24,56},{32,64},{40,72},{48,80},{56,88},{64,... | collective-permute-start | bytes 835592 | tf_op jit(solution)/shard_map/ppermute | solution.py:82
  16.8 17.4 %collective-permute-start.4 = (bf16[64,2176]{1,0:T(8,128)(2,1)S(1)}, bf16[64,2176]{1,0:T(8,128)(2,1)S(1)}, u32[]{:S(2)}, u32[]{:S(2)}) collective-permute-start(bf16[64,2176]{1,0:T(8,128)(2,1)S(1)} %pad_maximum_fusion.2.refs_0_), channel_id=1, source_target_pairs={{0,224},{8,232},{16,240},{24,248},{32,0},{40,8},{48,16},{56,24},{6... | collective-permute-start | bytes 835592 | tf_op jit(solution)/shard_map/ppermute | solution.py:82
  23.0 24.5 %collective-permute-start.7 = (bf16[64,2176]{1,0:T(8,128)(2,1)S(1)}, bf16[64,2176]{1,0:T(8,128)(2,1)S(1)}, u32[]{:S(2)}, u32[]{:S(2)}) collective-permute-start(bf16[64,2176]{1,0:T(8,128)(2,1)S(1)} %collective-permute-done.5.refs_3_), channel_id=1, source_target_pairs={{0,32},{8,40},{16,48},{24,56},{32,64},{40,72},{48,80},{56,88},{64,... | collective-permute-start | bytes 835592 | tf_op jit(solution)/shard_map/ppermute | solution.py:82
  29.2 18.4 %collective-permute-start.8 = (bf16[64,2176]{1,0:T(8,128)(2,1)S(1)}, bf16[64,2176]{1,0:T(8,128)(2,1)S(1)}, u32[]{:S(2)}, u32[]{:S(2)}) collective-permute-start(bf16[64,2176]{1,0:T(8,128)(2,1)S(1)} %collective-permute-done.6.refs_4_), channel_id=1, source_target_pairs={{0,224},{8,232},{16,240},{24,248},{32,0},{40,8},{48,16},{56,24},{6... | collective-permute-start | bytes 835592 | tf_op jit(solution)/shard_map/ppermute | solution.py:82
  29.9 20.0 %copy-start.1 = (bf16[1024,2048]{1,0:T(8,128)(2,1)S(1)}, bf16[1024,2048]{1,0:T(8,128)(2,1)}, u32[]{:S(2)}) copy-start(bf16[1024,2048]{1,0:T(8,128)(2,1)} %window.1) | copy-start | bytes 12582916
  29.9 17.6 %collective-permute-start.10 = (bf16[32,2176]{1,0:T(8,128)(2,1)S(1)}, bf16[32,2176]{1,0:T(8,128)(2,1)S(1)}, u32[]{:S(2)}, u32[]{:S(2)}) collective-permute-start(bf16[32,2176]{1,0:T(8,128)(2,1)S(1)} %slice.79), channel_id=1, source_target_pairs={{0,192},{8,200},{16,208},{24,216},{32,224},{40,232},{48,240},{56,2... | collective-permute-start | bytes 417800 | tf_op jit(solution)/shard_map/ppermute | solution.py:82
  34.1 13.5 %collective-permute-start.9 = (bf16[32,2176]{1,0:T(8,128)(2,1)S(1)}, bf16[32,2176]{1,0:T(8,128)(2,1)S(1)}, u32[]{:S(2)}, u32[]{:S(2)}) collective-permute-start(bf16[32,2176]{1,0:T(8,128)(2,1)S(1)} %slice.78), channel_id=1, source_target_pairs={{0,64},{8,72},{16,80},{24,88},{32,96},{40,104},{48,112},{56,120},{... | collective-permute-start | bytes 417800 | tf_op jit(solution)/shard_map/ppermute | solution.py:82
  53.4 12.3 %collective-permute-start.17 = (f32[4,128,512]{2,1,0:T(8,128)S(1)}, f32[4,128,512]{2,1,0:T(8,128)S(1)}, u32[]{:S(2)}, u32[]{:S(2)}) collective-permute-start(f32[4,128,512]{2,1,0:T(8,128)S(1)} %get-tuple-element.25), channel_id=1, source_target_pairs={{0,1},{1,0},{2,3},{3,2},{4,5},{5,4},{6,7},{7,6},{8,9},{9,8},{10,11... | collective-permute-start | bytes 3145736 | tf_op jit(solution)/shard_map/ppermute | solution.py:362
  55.1 2.1 %collective-permute-start.11 = (f32[2,320,128]{2,1,0:T(8,128)S(1)}, f32[2,320,128]{2,1,0:T(8,128)S(1)}, u32[]{:S(2)}, u32[]{:S(2)}) collective-permute-start(f32[2,320,128]{2,1,0:T(8,128)S(1)} %get-tuple-element.17), channel_id=1, source_target_pairs={{0,1},{1,0},{2,3},{3,2},{4,5},{5,4},{6,7},{7,6},{8,9},{9,8},{10,11... | collective-permute-start | bytes 983048 | tf_op jit(solution)/shard_map/ppermute | solution.py:362
  57.3 5.5 %collective-permute-start.12 = (f32[320,128]{1,0:T(8,128)S(1)}, f32[320,128]{1,0:T(8,128)S(1)}, u32[]{:S(2)}, u32[]{:S(2)}) collective-permute-start(f32[320,128]{1,0:T(8,128)S(1)} %get-tuple-element.31), channel_id=1, source_target_pairs={{0,2},{1,3},{2,0},{3,1},{4,6},{5,7},{6,4},{7,5},{8,10},{9,11},{10,... | collective-permute-start | bytes 491528 | tf_op jit(solution)/shard_map/ppermute | solution.py:371
  58.6 6.9 %collective-permute-start.14 = (f32[320,128]{1,0:T(8,128)S(1)}, f32[320,128]{1,0:T(8,128)S(1)}, u32[]{:S(2)}, u32[]{:S(2)}) collective-permute-start(f32[320,128]{1,0:T(8,128)S(1)} %get-tuple-element.32), channel_id=1, source_target_pairs={{0,6},{1,7},{2,4},{3,5},{4,2},{5,3},{6,0},{7,1},{8,14},{9,15},{10,... | collective-permute-start | bytes 491528 | tf_op jit(solution)/shard_map/ppermute | solution.py:371
  62.7 7.7 %collective-permute-start.13 = (f32[320,128]{1,0:T(8,128)S(1)}, f32[320,128]{1,0:T(8,128)S(1)}, u32[]{:S(2)}, u32[]{:S(2)}) collective-permute-start(f32[320,128]{1,0:T(8,128)S(1)} %add.96), channel_id=1, source_target_pairs={{0,6},{1,7},{2,4},{3,5},{4,2},{5,3},{6,0},{7,1},{8,14},{9,15},{10,... | collective-permute-start | bytes 491528 | tf_op jit(solution)/shard_map/ppermute | solution.py:372
  65.6 4.9 %collective-permute-start.15 = (f32[320,128]{1,0:T(8,128)S(1)}, f32[320,128]{1,0:T(8,128)S(1)}, u32[]{:S(2)}, u32[]{:S(2)}) collective-permute-start(f32[320,128]{1,0:T(8,128)S(1)} %add.100), channel_id=1, source_target_pairs={{0,2},{1,3},{2,0},{3,1},{4,6},{5,7},{6,4},{7,5},{8,10},{9,11},{10,... | collective-permute-start | bytes 491528 | tf_op jit(solution)/shard_map/ppermute | solution.py:372
  65.9 8.5 %collective-permute-start.18 = (f32[128,512]{1,0:T(8,128)S(1)}, f32[128,512]{1,0:T(8,128)S(1)}, u32[]{:S(2)}, u32[]{:S(2)}) collective-permute-start(f32[128,512]{1,0:T(8,128)S(1)} %get-tuple-element.30), channel_id=1, source_target_pairs={{0,2},{1,3},{2,4},{3,5},{4,6},{5,7},{6,0},{7,1},{8,10},{9,11},{10,... | collective-permute-start | bytes 786440 | tf_op jit(solution)/shard_map/ppermute | solution.py:363
  67.4 14.8 %collective-permute-start.19 = (f32[128,512]{1,0:T(8,128)S(1)}, f32[128,512]{1,0:T(8,128)S(1)}, u32[]{:S(2)}, u32[]{:S(2)}) collective-permute-start(f32[128,512]{1,0:T(8,128)S(1)} %get-tuple-element.28), channel_id=1, source_target_pairs={{0,4},{1,5},{2,6},{3,7},{4,0},{5,1},{6,2},{7,3},{8,12},{9,13},{10,... | collective-permute-start | bytes 786440 | tf_op jit(solution)/shard_map/ppermute | solution.py:363
  68.5 13.7 %collective-permute-start.20 = (f32[128,512]{1,0:T(8,128)S(1)}, f32[128,512]{1,0:T(8,128)S(1)}, u32[]{:S(2)}, u32[]{:S(2)}) collective-permute-start(f32[128,512]{1,0:T(8,128)S(1)} %get-tuple-element.29), channel_id=1, source_target_pairs={{0,6},{1,7},{2,0},{3,1},{4,2},{5,3},{6,4},{7,5},{8,14},{9,15},{10,... | collective-permute-start | bytes 786440 | tf_op jit(solution)/shard_map/ppermute | solution.py:363
  82.3 6.5 %collective-permute-start.21 = (f32[128,512]{1,0:T(8,128)S(1)}, f32[128,512]{1,0:T(8,128)S(1)}, u32[]{:S(2)}, u32[]{:S(2)}) collective-permute-start(f32[128,512]{1,0:T(8,128)S(1)} %fusion.5), channel_id=1, source_target_pairs={{0,2},{1,3},{2,4},{3,5},{4,6},{5,7},{6,0},{7,1},{8,10},{9,11},{10,... | collective-permute-start | bytes 786440 | tf_op jit(solution)/shard_map/ppermute | solution.py:363
  82.9 13.0 %collective-permute-start.22 = (f32[128,512]{1,0:T(8,128)S(1)}, f32[128,512]{1,0:T(8,128)S(1)}, u32[]{:S(2)}, u32[]{:S(2)}) collective-permute-start(f32[128,512]{1,0:T(8,128)S(1)} %fusion.5), channel_id=1, source_target_pairs={{0,4},{1,5},{2,6},{3,7},{4,0},{5,1},{6,2},{7,3},{8,12},{9,13},{10,... | collective-permute-start | bytes 786440 | tf_op jit(solution)/shard_map/ppermute | solution.py:363
  85.2 11.7 %collective-permute-start.23 = (f32[128,512]{1,0:T(8,128)S(1)}, f32[128,512]{1,0:T(8,128)S(1)}, u32[]{:S(2)}, u32[]{:S(2)}) collective-permute-start(f32[128,512]{1,0:T(8,128)S(1)} %fusion.5), channel_id=1, source_target_pairs={{0,6},{1,7},{2,0},{3,1},{4,2},{5,3},{6,4},{7,5},{8,14},{9,15},{10,... | collective-permute-start | bytes 786440 | tf_op jit(solution)/shard_map/ppermute | solution.py:363
  85.4 13.6 %collective-permute-start.16 = (f32[2,320,128]{2,1,0:T(8,128)S(1)}, f32[2,320,128]{2,1,0:T(8,128)S(1)}, u32[]{:S(2)}, u32[]{:S(2)}) collective-permute-start(f32[2,320,128]{2,1,0:T(8,128)S(1)} %pad_maximum_fusion.1.near), channel_id=1, source_target_pairs={{0,1},{1,0},{2,3},{3,2},{4,5},{5,4},{6,7},{7,6},{8,9},{9,8},{10,11... | collective-permute-start | bytes 983048 | tf_op jit(solution)/shard_map/ppermute | solution.py:362
  97.0 22.5 %collective-permute-start.24 = (f32[4,128,512]{2,1,0:T(8,128)S(1)}, f32[4,128,512]{2,1,0:T(8,128)S(1)}, u32[]{:S(2)}, u32[]{:S(2)}) collective-permute-start(f32[4,128,512]{2,1,0:T(8,128)S(1)} %pad_maximum_fusion.near), channel_id=1, source_target_pairs={{0,1},{1,0},{2,3},{3,2},{4,5},{5,4},{6,7},{7,6},{8,9},{9,8},{10,11... | collective-permute-start | bytes 3145736 | tf_op jit(solution)/shard_map/ppermute | solution.py:362
  109.0 10.5 %copy-start = (bf16[1024,64]{0,1:T(8,128)(2,1)S(1)}, bf16[1024,64]{0,1:T(8,128)(2,1)}, u32[]{:S(2)}) copy-start(bf16[1024,64]{0,1:T(8,128)(2,1)} %param.10) | copy-start | bytes 393220

commit v2 on v1

--- a/solution.py
+++ b/solution.py
@@ -86,10 +86,9 @@
     return [own, up1, down1, up2, down2, up3, down3, up4, down4]
 
 
-def gram_kernel(*refs):
-    pieces, (rows, sides, other, mine, blocks) = refs[:9], refs[9:]
-    z, x, _, c = place()
-    for piece, (turn, first) in zip(pieces, PIECES):
+def sort_rows(pieces, places, rows, sides):
+    z, x, _, _ = place()
+    for piece, (turn, first) in zip(pieces, places):
 
         @pl.loop(0, piece.shape[0] // 16)
         def _(i):
@@ -99,14 +98,37 @@
             rows[at] = held[:, :2048]
             sides[at] = held[:, 2048:]
 
-    at = 0
-    for i in range(4):
+
+SORTED = (jax.ShapeDtypeStruct((COUNT, 2048), BF16), jax.ShapeDtypeStruct((COUNT, 128), BF16))
+
+
+def early_kernel(*refs):
+    sort_rows(refs[:5], PIECES[:5], *refs[5:])
+
+
+def early(pieces):
+    return pl.pallas_call(
+        early_kernel,
+        name="early",
+        out_shape=SORTED,
+        in_specs=[VMEM] * 5,
+        out_specs=(VMEM, VMEM),
+        compiler_params=grant(4),
+        cost_estimate=pl.CostEstimate(flops=10**6, bytes_accessed=2 << 20, transcendentals=0),
+    )(*pieces)
+
+
+def gram_kernel(rows_in, sides_in, up3, down3, up4, down4, rows, sides, other, mine, blocks):
+    _, _, _, c = place()
+    sort_rows((up3, down3, up4, down4), PIECES[5:], rows, sides)
+    for half in range(2):
         part = lax.dot_general(
-            rows[128 * i : 128 * i + 128], rows[: 128 * i + 128], (NT, ((), ())), preferred_element_type=F32
+            rows[256 * half :], rows[256 * half : 256 * half + 256], (NT, ((), ())), preferred_element_type=F32
         )
-        for j in range(i + 1):
-            blocks[at] = part[:, 128 * j : 128 * j + 128]
-            at += 1
+        for b, (i, j) in enumerate(BLOCKS):
+            if j // 2 == half:
+                at = 128 * i - 256 * half
+                blocks[b] = part[at : at + 128, 128 * (j % 2) : 128 * (j % 2) + 128]
     for n in range(2):
         for out, core in ((other, 1 - c), (mine, c)):
             first = pl.multiple_of(64 * core + 32 * n, 32)
@@ -114,54 +136,43 @@
                 out[n, 32 * b : 32 * b + 32] = blocks[b, pl.ds(first, 32), :]
 
 
-def gram(pieces):
+def gram(rows, sides, pieces):
     chunk = jax.ShapeDtypeStruct((2, 32 * len(BLOCKS), 128), F32)
     return pl.pallas_call(
         gram_kernel,
         name="gram",
-        out_shape=(
-            jax.ShapeDtypeStruct((COUNT, 2048), BF16),
-            jax.ShapeDtypeStruct((COUNT, 128), BF16),
-            chunk,
-            chunk,
-        ),
-        in_specs=[VMEM] * 9,
+        out_shape=(*SORTED, chunk, chunk),
+        in_specs=[VMEM] * 6,
         out_specs=(VMEM,) * 4,
+        input_output_aliases={0: 0, 1: 1},
         scratch_shapes=[pltpu.VMEM((len(BLOCKS), 128, 128), F32)],
         compiler_params=grant(10),
         cost_estimate=pl.CostEstimate(flops=2 * COUNT * COUNT * 2048, bytes_accessed=2 << 20, transcendentals=0),
-    )(*pieces)
+    )(rows, sides, *pieces)
 
 
 def schur_kernel(window, rows, other, mine, held, sem):
     _, _, y, c = place()
 
     def fetch(i):
-        slot = lax.rem(i, 2)
-        core = jnp.where(i < 2, 1 - c, c)
-        first = pl.multiple_of(512 * core + 256 * slot, 256)
-        return pltpu.make_async_copy(window.at[pl.ds(first, 256)], held.at[slot], sem.at[slot])
-
-    fetch(0).start()
-
-    @pl.loop(0, 4)
-    def _(i):
-        @pl.when(i < 3)
-        def _():
-            fetch(i + 1).start()
-
-        fetch(i).wait()
-        part = lax.dot_general(held[lax.rem(i, 2)], rows[...], (NT, ((), ())), preferred_element_type=F32)
+        core = 1 - c if i < 2 else c
+        first = pl.multiple_of(512 * core + 256 * (i % 2), 256)
+        return pltpu.make_async_copy(window.at[pl.ds(first, 256)], held.at[pl.ds(256 * i, 256)], sem.at[i])
+
+    for i in range(4):
+        fetch(i).start()
+    for half, out in enumerate((other, mine)):
+        for i in range(2):
+            fetch(2 * half + i).wait()
         for n in range(2):
-            k = lax.rem(2 * lax.rem(i, 2) + n - y + NY, NY)
-
-            @pl.when(i < 2)
-            def _():
-                other[k] = part[128 * n : 128 * n + 128]
-
-            @pl.when(i >= 2)
-            def _():
-                mine[k] = part[128 * n : 128 * n + 128]
+            part = lax.dot_general(
+                held[512 * half : 512 * half + 512],
+                rows[256 * n : 256 * n + 256],
+                (NT, ((), ())),
+                preferred_element_type=F32,
+            )
+            for i in range(NY):
+                out[lax.rem(i - y + NY, NY), :, 256 * n : 256 * n + 256] = part[128 * i : 128 * i + 128]
 
 
 def schur(window, rows):
@@ -172,7 +183,7 @@
         out_shape=(chunk, chunk),
         in_specs=[pl.BlockSpec(memory_space=pltpu.HBM), VMEM],
         out_specs=(VMEM, VMEM),
-        scratch_shapes=[pltpu.VMEM((2, 256, 2048), BF16), pltpu.SemaphoreType.DMA((2,))],
+        scratch_shapes=[pltpu.VMEM((1024, 2048), BF16), pltpu.SemaphoreType.DMA((4,))],
         compiler_params=grant(12),
         cost_estimate=pl.CostEstimate(flops=2 * 1024 * COUNT * 2048, bytes_accessed=8 << 20, transcendentals=0),
     )(window, rows)
@@ -365,7 +376,7 @@
     held = jnp.concatenate([pivot_factor, pivot_sides, jnp.zeros_like(pivot_sides)], axis=1)
     near = [held] + [lax.ppermute(held, "row", shift_x(k)) for k in (1, 2, 3)]
     pieces = tower(jnp.concatenate(near, axis=0))
-    rows, sides, gram_other, gram_mine = gram(pieces)
+    rows, sides, gram_other, gram_mine = gram(*early(pieces[:5]), pieces[5:])
     gram_far = swap(gram_other)
     sums = [gram_mine[n] + gram_far[n] for n in range(2)]
     sums = [sums[n] + lax.ppermute(sums[n], "layer", PAIRS[n]) for n in range(2)]

time: 121 us -> 120 us (level)
  Pallas kernels: 28 us -> 26.7 us
where the time goes in v2:
time: 120 us
  waiting for transfers between devices  46.8 us (39%)
  starting transfers between devices  41.5 us (35%)
  Pallas kernels  26.7 us (22%)
  other arithmetic  2.89 us (2%)
    ppermute x8, waiting for transfers between devices, tower(): hop = lambda a, k: lax.ppermute(a, 'row', shift_z(k))  21 us
    ppermute x6, waiting for transfers between devices, shards(): along = lambda a, k: lax.ppermute(a, 'layer', shift_y(k))  20.2 us
    ppermute x8, starting transfers between devices, tower(): hop = lambda a, k: lax.ppermute(a, 'row', shift_z(k))  16.1 us
    pallas_call x1, Pallas kernels, weigh(): pl.pallas_call(weights_kernel, name='weigh', out_shape=(square, square, j...  10.4 us
    pallas_call x1, Pallas kernels, factor(): pl.pallas_call(factor_kernel, name='factor', out_shape=(square, square),...  10 us
    ppermute x6, starting transfers between devices, shards(): along = lambda a, k: lax.ppermute(a, 'layer', shift_y(k))  7.62 us
    ppermute x4, starting transfers between devices, shards(): swap = lambda a: lax.ppermute(a, 'layer', SWAP)  6.02 us
    ppermute x3, starting transfers between devices, shards(): near = [held] + [lax.ppermute(held, 'row', shift_x(k)) for k in (1, 2, 3)]  5.64 us
  transfers between devices with their start and end apart: 25, of which 14 were waited for; matrix products, arithmetic and copies ran while one was open for 2% of the time, Pallas kernels for 17%

profile of v2, /device:TPU:1, one launch (start us, length us, event | category | flops | bytes accessed | tf_op | source)
XLA Modules:
  0.0 119.7 jit_solution(5687823066987330839)
XLA Ops:
  0.6 0.9 concatenate.6
  1.6 2.0 %collective-permute-start = (bf16[16,2176]{1,0:T(8,128)(2,1)S(1)}, bf16[16,2176]{1,0:T(8,128)(2,1)S(1)}, u32[]{:S(2)}, u32[]{:S(2)}) collective-permute-start(bf16[16,2176]{1,0:T(8,128)(2,1)S(1)} %concatenate.6), channel_id=1, source_target_pairs={{0,8},{8,16},{16,24},{24,0},{32,40},{40,48},{48,56},{56,32},{64,72... | collective-permute-start | bytes 208904 | tf_op jit(solution)/shard_map/ppermute | solution.py:377
  3.6 2.5 %collective-permute-start.1 = (bf16[16,2176]{1,0:T(8,128)(2,1)S(1)}, bf16[16,2176]{1,0:T(8,128)(2,1)S(1)}, u32[]{:S(2)}, u32[]{:S(2)}) collective-permute-start(bf16[16,2176]{1,0:T(8,128)(2,1)S(1)} %concatenate.6), channel_id=1, source_target_pairs={{0,16},{8,24},{16,0},{24,8},{32,48},{40,56},{48,32},{56,40},{64,80... | collective-permute-start | bytes 208904 | tf_op jit(solution)/shard_map/ppermute | solution.py:377
  6.1 1.2 collective-permute-start.2
  7.2 0.0 collective-permute-done
  7.2 1.6 %collective-permute-done.1 = bf16[16,2176]{1,0:T(8,128)(2,1)S(1)} collective-permute-done((bf16[16,2176]{1,0:T(8,128)(2,1)S(1)}, bf16[16,2176]{1,0:T(8,128)(2,1)S(1)}, u32[]{:S(2)}, u32[]{:S(2)}) %collective-permute-start.1) | collective-permute-done | bytes 69664 | tf_op jit(solution)/shard_map/ppermute | solution.py:377
  8.9 0.7 collective-permute-done.2
  9.5 3.4 %collective-permute-start.5 = (bf16[64,2176]{1,0:T(8,128)(2,1)S(1)}, bf16[64,2176]{1,0:T(8,128)(2,1)S(1)}, u32[]{:S(2)}, u32[]{:S(2)}) collective-permute-start(bf16[64,2176]{1,0:T(8,128)(2,1)S(1)} %pad_maximum_fusion.2.refs_0_), channel_id=1, source_target_pairs={{0,64},{8,72},{16,80},{24,88},{32,96},{40,104},{48,112},{56,120},{... | collective-permute-start | bytes 835592 | tf_op jit(solution)/shard_map/ppermute | solution.py:82
  12.9 3.1 %collective-permute-start.6 = (bf16[64,2176]{1,0:T(8,128)(2,1)S(1)}, bf16[64,2176]{1,0:T(8,128)(2,1)S(1)}, u32[]{:S(2)}, u32[]{:S(2)}) collective-permute-start(bf16[64,2176]{1,0:T(8,128)(2,1)S(1)} %pad_maximum_fusion.2.refs_0_), channel_id=1, source_target_pairs={{0,192},{8,200},{16,208},{24,216},{32,224},{40,232},{48,240},{56,2... | collective-permute-start | bytes 835592 | tf_op jit(solution)/shard_map/ppermute | solution.py:82
  16.0 0.7 collective-permute-start.3
  16.8 1.9 %collective-permute-start.4 = (bf16[64,2176]{1,0:T(8,128)(2,1)S(1)}, bf16[64,2176]{1,0:T(8,128)(2,1)S(1)}, u32[]{:S(2)}, u32[]{:S(2)}) collective-permute-start(bf16[64,2176]{1,0:T(8,128)(2,1)S(1)} %pad_maximum_fusion.2.refs_0_), channel_id=1, source_target_pairs={{0,224},{8,232},{16,240},{24,248},{32,0},{40,8},{48,16},{56,24},{6... | collective-permute-start | bytes 835592 | tf_op jit(solution)/shard_map/ppermute | solution.py:82
  18.7 4.3 %collective-permute-done.5.refs_3_ = bf16[64,2176]{1,0:T(8,128)(2,1)S(1)} collective-permute-done((bf16[64,2176]{1,0:T(8,128)(2,1)S(1)}, bf16[64,2176]{1,0:T(8,128)(2,1)S(1)}, u32[]{:S(2)}, u32[]{:S(2)}) %collective-permute-start.5) | collective-permute-done | bytes 278560 | tf_op jit(solution)/shard_map/ppermute | solution.py:82
  23.0 5.4 %collective-permute-start.7 = (bf16[64,2176]{1,0:T(8,128)(2,1)S(1)}, bf16[64,2176]{1,0:T(8,128)(2,1)S(1)}, u32[]{:S(2)}, u32[]{:S(2)}) collective-permute-start(bf16[64,2176]{1,0:T(8,128)(2,1)S(1)} %collective-permute-done.5.refs_3_), channel_id=1, source_target_pairs={{0,32},{8,40},{16,48},{24,56},{32,64},{40,72},{48,80},{56,88},{64,... | collective-permute-start | bytes 835592 | tf_op jit(solution)/shard_map/ppermute | solution.py:82
  28.4 0.8 collective-permute-done.6.refs_4_
  29.2 0.0 collective-permute-start.8
  29.2 0.7 convert_element_type.4
  29.9 1.5 %collective-permute-start.10 = (bf16[32,2176]{1,0:T(8,128)(2,1)S(1)}, bf16[32,2176]{1,0:T(8,128)(2,1)S(1)}, u32[]{:S(2)}, u32[]{:S(2)}) collective-permute-start(bf16[32,2176]{1,0:T(8,128)(2,1)S(1)} %slice.79), channel_id=1, source_target_pairs={{0,192},{8,200},{16,208},{24,216},{32,224},{40,232},{48,240},{56,2... | collective-permute-start | bytes 417800 | tf_op jit(solution)/shard_map/ppermute | solution.py:82
  31.5 2.6 %collective-permute-done.3.refs_1_ = bf16[64,2176]{1,0:T(8,128)(2,1)S(1)} collective-permute-done((bf16[64,2176]{1,0:T(8,128)(2,1)S(1)}, bf16[64,2176]{1,0:T(8,128)(2,1)S(1)}, u32[]{:S(2)}, u32[]{:S(2)}) %collective-permute-start.3) | collective-permute-done | bytes 278560 | tf_op jit(solution)/shard_map/ppermute | solution.py:82
  34.1 0.0 collective-permute-start.9
  34.1 0.1 collective-permute-done.4.refs_2_
  34.2 0.3 early.1
  34.5 13.1 %collective-permute-done.10.down4 = bf16[32,2176]{1,0:T(8,128)(2,1)S(1)} collective-permute-done((bf16[32,2176]{1,0:T(8,128)(2,1)S(1)}, bf16[32,2176]{1,0:T(8,128)(2,1)S(1)}, u32[]{:S(2)}, u32[]{:S(2)}) %collective-permute-start.10) | collective-permute-done | bytes 139296 | tf_op jit(solution)/shard_map/ppermute | solution.py:82
  47.6 0.0 collective-permute-done.9.up4
  47.6 0.0 collective-permute-done.7.up3
  47.6 0.0 collective-permute-done.8.down3
  47.6 1.3 %gram.1 = (bf16[512,2048]{1,0:T(8,128)(2,1)S(1)}, bf16[512,128]{1,0:T(8,128)(2,1)S(1)}, f32[2,320,128]{2,1,0:T(8,128)S(1)}, f32[2,320,128]{2,1,0:T(8,128)S(1)}) custom-call(bf16[512,2048]{1,0:T(8,128)(2,1)S(1)} %get-tuple-element.18.rows_in, bf16[512,128]{1,0:T(8,128)(2,1)S(1)} %get-tuple-element.19.sides_in, ...), custom_call_target="tpu_custom_call", output_to_operand_aliasing={{0}: (0, {}), {1}: (1, {})} | custom-call | flops 1073741824 | bytes 2097152 | tf_op jit(solution)/shard_map/gram/pallas_call | solution.py:141
  48.9 2.9 %schur.1 = (f32[4,128,512]{2,1,0:T(8,128)S(1)}, f32[4,128,512]{2,1,0:T(8,128)S(1)}) custom-call(bf16[1024,2048]{1,0:T(8,128)(2,1)S(1)} %copy-done.1, bf16[512,2048]{1,0:T(8,128)(2,1)S(1)} %get-tuple-element.27.rows), custom_call_target="tpu_custom_call" | custom-call | flops 2147483648 | bytes 8388608 | tf_op jit(solution)/shard_map/schur/pallas_call | solution.py:180
  51.8 1.1 collective-permute-start.17
  52.9 0.7 dynamic-slice_convert_fusion
  53.6 0.0 collective-permute-start.11
  53.6 0.7 select_add_fusion.cov
  54.4 1.3 %collective-permute-done.11 = f32[2,320,128]{2,1,0:T(8,128)S(1)} collective-permute-done((f32[2,320,128]{2,1,0:T(8,128)S(1)}, f32[2,320,128]{2,1,0:T(8,128)S(1)}, u32[]{:S(2)}, u32[]{:S(2)}) %collective-permute-start.11) | collective-permute-done | bytes 327712 | tf_op jit(solution)/shard_map/ppermute | solution.py:373
  55.7 0.1 fusion.7
  55.7 1.4 %collective-permute-start.12 = (f32[320,128]{1,0:T(8,128)S(1)}, f32[320,128]{1,0:T(8,128)S(1)}, u32[]{:S(2)}, u32[]{:S(2)}) collective-permute-start(f32[320,128]{1,0:T(8,128)S(1)} %get-tuple-element.35), channel_id=1, source_target_pairs={{0,2},{1,3},{2,0},{3,1},{4,6},{5,7},{6,4},{7,5},{8,10},{9,11},{10,... | collective-permute-start | bytes 491528 | tf_op jit(solution)/shard_map/ppermute | solution.py:382
  57.1 1.9 %collective-permute-start.14 = (f32[320,128]{1,0:T(8,128)S(1)}, f32[320,128]{1,0:T(8,128)S(1)}, u32[]{:S(2)}, u32[]{:S(2)}) collective-permute-start(f32[320,128]{1,0:T(8,128)S(1)} %get-tuple-element.36), channel_id=1, source_target_pairs={{0,6},{1,7},{2,4},{3,5},{4,2},{5,3},{6,0},{7,1},{8,14},{9,15},{10,... | collective-permute-start | bytes 491528 | tf_op jit(solution)/shard_map/ppermute | solution.py:382
  59.0 0.2 exponential_multiply_fusion
  59.2 2.0 %collective-permute-done.12 = f32[320,128]{1,0:T(8,128)S(1)} collective-permute-done((f32[320,128]{1,0:T(8,128)S(1)}, f32[320,128]{1,0:T(8,128)S(1)}, u32[]{:S(2)}, u32[]{:S(2)}) %collective-permute-start.12) | collective-permute-done | bytes 163872 | tf_op jit(solution)/shard_map/ppermute | solution.py:382
  61.2 2.8 %collective-permute-start.13 = (f32[320,128]{1,0:T(8,128)S(1)}, f32[320,128]{1,0:T(8,128)S(1)}, u32[]{:S(2)}, u32[]{:S(2)}) collective-permute-start(f32[320,128]{1,0:T(8,128)S(1)} %add.96), channel_id=1, source_target_pairs={{0,6},{1,7},{2,4},{3,5},{4,2},{5,3},{6,0},{7,1},{8,14},{9,15},{10,... | collective-permute-start | bytes 491528 | tf_op jit(solution)/shard_map/ppermute | solution.py:383
  64.0 0.0 collective-permute-done.14
  64.0 0.1 collective-permute-start.15
  64.1 0.0 collective-permute-done.17
  64.2 0.1 fusion.1
  64.3 1.5 %collective-permute-start.18 = (f32[128,512]{1,0:T(8,128)S(1)}, f32[128,512]{1,0:T(8,128)S(1)}, u32[]{:S(2)}, u32[]{:S(2)}) collective-permute-start(f32[128,512]{1,0:T(8,128)S(1)} %get-tuple-element.34), channel_id=1, source_target_pairs={{0,2},{1,3},{2,4},{3,5},{4,6},{5,7},{6,0},{7,1},{8,10},{9,11},{10,... | collective-permute-start | bytes 786440 | tf_op jit(solution)/shard_map/ppermute | solution.py:374
  65.8 1.1 collective-permute-start.19
  66.9 2.0 %collective-permute-start.20 = (f32[128,512]{1,0:T(8,128)S(1)}, f32[128,512]{1,0:T(8,128)S(1)}, u32[]{:S(2)}, u32[]{:S(2)}) collective-permute-start(f32[128,512]{1,0:T(8,128)S(1)} %get-tuple-element.33), channel_id=1, source_target_pairs={{0,6},{1,7},{2,0},{3,1},{4,2},{5,3},{6,4},{7,5},{8,14},{9,15},{10,... | collective-permute-start | bytes 786440 | tf_op jit(solution)/shard_map/ppermute | solution.py:374
  68.9 0.0 collective-permute-done.15
  69.0 3.8 %collective-permute-done.18 = f32[128,512]{1,0:T(8,128)S(1)} collective-permute-done((f32[128,512]{1,0:T(8,128)S(1)}, f32[128,512]{1,0:T(8,128)S(1)}, u32[]{:S(2)}, u32[]{:S(2)}) %collective-permute-start.18) | collective-permute-done | bytes 262176 | tf_op jit(solution)/shard_map/ppermute | solution.py:374
  72.8 7.8 %collective-permute-done.19 = f32[128,512]{1,0:T(8,128)S(1)} collective-permute-done((f32[128,512]{1,0:T(8,128)S(1)}, f32[128,512]{1,0:T(8,128)S(1)}, u32[]{:S(2)}, u32[]{:S(2)}) %collective-permute-start.19) | collective-permute-done | bytes 262176 | tf_op jit(solution)/shard_map/ppermute | solution.py:374
  80.6 0.2 fusion.5
  80.8 0.5 collective-permute-start.21
  81.3 2.4 %collective-permute-start.22 = (f32[128,512]{1,0:T(8,128)S(1)}, f32[128,512]{1,0:T(8,128)S(1)}, u32[]{:S(2)}, u32[]{:S(2)}) collective-permute-start(f32[128,512]{1,0:T(8,128)S(1)} %fusion.5), channel_id=1, source_target_pairs={{0,4},{1,5},{2,6},{3,7},{4,0},{5,1},{6,2},{7,3},{8,12},{9,13},{10,... | collective-permute-start | bytes 786440 | tf_op jit(solution)/shard_map/ppermute | solution.py:374
  83.7 0.1 collective-permute-start.23
  83.8 2.9 %collective-permute-start.16 = (f32[2,320,128]{2,1,0:T(8,128)S(1)}, f32[2,320,128]{2,1,0:T(8,128)S(1)}, u32[]{:S(2)}, u32[]{:S(2)}) collective-permute-start(f32[2,320,128]{2,1,0:T(8,128)S(1)} %pad_maximum_fusion.1.near), channel_id=1, source_target_pairs={{0,1},{1,0},{2,3},{3,2},{4,5},{5,4},{6,7},{7,6},{8,9},{9,8},{10,11... | collective-permute-start | bytes 983048 | tf_op jit(solution)/shard_map/ppermute | solution.py:373
  86.8 0.5 collective-permute-done.21
  87.3 7.0 %collective-permute-done.22 = f32[128,512]{1,0:T(8,128)S(1)} collective-permute-done((f32[128,512]{1,0:T(8,128)S(1)}, f32[128,512]{1,0:T(8,128)S(1)}, u32[]{:S(2)}, u32[]{:S(2)}) %collective-permute-start.22) | collective-permute-done | bytes 262176 | tf_op jit(solution)/shard_map/ppermute | solution.py:374
  94.3 1.1 collective-permute-done.23
  95.3 0.1 pad_maximum_fusion.near
  95.4 2.0 %collective-permute-start.24 = (f32[4,128,512]{2,1,0:T(8,128)S(1)}, f32[4,128,512]{2,1,0:T(8,128)S(1)}, u32[]{:S(2)}, u32[]{:S(2)}) collective-permute-start(f32[4,128,512]{2,1,0:T(8,128)S(1)} %pad_maximum_fusion.near), channel_id=1, source_target_pairs={{0,1},{1,0},{2,3},{3,2},{4,5},{5,4},{6,7},{7,6},{8,9},{9,8},{10,11... | collective-permute-start | bytes 3145736 | tf_op jit(solution)/shard_map/ppermute | solution.py:373
  97.4 0.0 collective-permute-done.16.far
  97.4 10.0 %factor.1 = (f32[512,512]{1,0:T(8,128)S(1)}, f32[512,512]{1,0:T(8,128)S(1)}) custom-call(f32[512,512]{1,0:T(8,128)S(1)} %select_add_fusion.cov, f32[2,320,128]{2,1,0:T(8,128)S(1)} %pad_maximum_fusion.1.near, f32[2,320,128]{2,1,0:T(8,128)S(1)} %collective-permute-done.16.far), custom_call_target="tpu_custom_call" | custom-call | flops 10000000000 | bytes 4194304 | tf_op jit(solution)/shard_map/factor/pallas_call | solution.py:312
  107.5 0.0 copy-start
  107.5 10.4 %weigh.1 = (f32[512,512]{1,0:T(8,128)S(1)}, f32[512,512]{1,0:T(8,128)S(1)}, f32[128,512]{1,0:T(8,128)S(1)}) custom-call(f32[512,512]{1,0:T(8,128)S(1)} %get-tuple-element.22.a_in, f32[512,512]{1,0:T(8,128)S(1)} %get-tuple-element.23.e_in, bf16[512,128]{1,0:T(8,128)(2,1)S(1)} %get-tuple-element.24.sides), custom_call_target="tpu_custom_call", output_to_operand_aliasing={{0}: (0, {}), {1}: (1, {})} | custom-call | flops 10000000000 | bytes 4194304 | tf_op jit(solution)/shard_map/weigh/pallas_call | solution.py:335
  117.9 0.0 collective-permute-done.24.far
  117.9 1.8 %finish.1 = (f32[64,1024]{1,0:T(8,128)}, f32[64,1024]{1,0:T(8,128)}) custom-call(f32[128,512]{1,0:T(8,128)S(1)} %get-tuple-element.25.weights, f32[4,128,512]{2,1,0:T(8,128)S(1)} %pad_maximum_fusion.near, f32[4,128,512]{2,1,0:T(8,128)S(1)} %collective-permute-done.24.far, bf16[64,1024]{1,0:T(8,128)(2,1)S(1)} %bitcast.33), custom_call_target="tpu_custom_call" | custom-call | flops 402653184 | bytes 3145728 | tf_op jit(solution)/shard_map/finish/pallas_call | solution.py:360
  (16 shorter events, 0.2 us)
Async XLA Ops:
  1.6 5.6 %collective-permute-start = (bf16[16,2176]{1,0:T(8,128)(2,1)S(1)}, bf16[16,2176]{1,0:T(8,128)(2,1)S(1)}, u32[]{:S(2)}, u32[]{:S(2)}) collective-permute-start(bf16[16,2176]{1,0:T(8,128)(2,1)S(1)} %concatenate.6), channel_id=1, source_target_pairs={{0,8},{8,16},{16,24},{24,0},{32,40},{40,48},{48,56},{56,32},{64,72... | collective-permute-start | bytes 208904 | tf_op jit(solution)/shard_map/ppermute | solution.py:377
  3.6 5.2 %collective-permute-start.1 = (bf16[16,2176]{1,0:T(8,128)(2,1)S(1)}, bf16[16,2176]{1,0:T(8,128)(2,1)S(1)}, u32[]{:S(2)}, u32[]{:S(2)}) collective-permute-start(bf16[16,2176]{1,0:T(8,128)(2,1)S(1)} %concatenate.6), channel_id=1, source_target_pairs={{0,16},{8,24},{16,0},{24,8},{32,48},{40,56},{48,32},{56,40},{64,80... | collective-permute-start | bytes 208904 | tf_op jit(solution)/shard_map/ppermute | solution.py:377
  6.1 3.5 %collective-permute-start.2 = (bf16[16,2176]{1,0:T(8,128)(2,1)S(1)}, bf16[16,2176]{1,0:T(8,128)(2,1)S(1)}, u32[]{:S(2)}, u32[]{:S(2)}) collective-permute-start(bf16[16,2176]{1,0:T(8,128)(2,1)S(1)} %concatenate.6), channel_id=1, source_target_pairs={{0,24},{8,0},{16,8},{24,16},{32,56},{40,32},{48,40},{56,48},{64,88... | collective-permute-start | bytes 208904 | tf_op jit(solution)/shard_map/ppermute | solution.py:377
  9.5 13.5 %collective-permute-start.5 = (bf16[64,2176]{1,0:T(8,128)(2,1)S(1)}, bf16[64,2176]{1,0:T(8,128)(2,1)S(1)}, u32[]{:S(2)}, u32[]{:S(2)}) collective-permute-start(bf16[64,2176]{1,0:T(8,128)(2,1)S(1)} %pad_maximum_fusion.2.refs_0_), channel_id=1, source_target_pairs={{0,64},{8,72},{16,80},{24,88},{32,96},{40,104},{48,112},{56,120},{... | collective-permute-start | bytes 835592 | tf_op jit(solution)/shard_map/ppermute | solution.py:82
  12.9 16.3 %collective-permute-start.6 = (bf16[64,2176]{1,0:T(8,128)(2,1)S(1)}, bf16[64,2176]{1,0:T(8,128)(2,1)S(1)}, u32[]{:S(2)}, u32[]{:S(2)}) collective-permute-start(bf16[64,2176]{1,0:T(8,128)(2,1)S(1)} %pad_maximum_fusion.2.refs_0_), channel_id=1, source_target_pairs={{0,192},{8,200},{16,208},{24,216},{32,224},{40,232},{48,240},{56,2... | collective-permute-start | bytes 835592 | tf_op jit(solution)/shard_map/ppermute | solution.py:82
  16.0 18.1 %collective-permute-start.3 = (bf16[64,2176]{1,0:T(8,128)(2,1)S(1)}, bf16[64,2176]{1,0:T(8,128)(2,1)S(1)}, u32[]{:S(2)}, u32[]{:S(2)}) collective-permute-start(bf16[64,2176]{1,0:T(8,128)(2,1)S(1)} %pad_maximum_fusion.2.refs_0_), channel_id=1, source_target_pairs={{0,32},{8,40},{16,48},{24,56},{32,64},{40,72},{48,80},{56,88},{64,... | collective-permute-start | bytes 835592 | tf_op jit(solution)/shard_map/ppermute | solution.py:82
  16.8 17.4 %collective-permute-start.4 = (bf16[64,2176]{1,0:T(8,128)(2,1)S(1)}, bf16[64,2176]{1,0:T(8,128)(2,1)S(1)}, u32[]{:S(2)}, u32[]{:S(2)}) collective-permute-start(bf16[64,2176]{1,0:T(8,128)(2,1)S(1)} %pad_maximum_fusion.2.refs_0_), channel_id=1, source_target_pairs={{0,224},{8,232},{16,240},{24,248},{32,0},{40,8},{48,16},{56,24},{6... | collective-permute-start | bytes 835592 | tf_op jit(solution)/shard_map/ppermute | solution.py:82
  23.0 24.5 %collective-permute-start.7 = (bf16[64,2176]{1,0:T(8,128)(2,1)S(1)}, bf16[64,2176]{1,0:T(8,128)(2,1)S(1)}, u32[]{:S(2)}, u32[]{:S(2)}) collective-permute-start(bf16[64,2176]{1,0:T(8,128)(2,1)S(1)} %collective-permute-done.5.refs_3_), channel_id=1, source_target_pairs={{0,32},{8,40},{16,48},{24,56},{32,64},{40,72},{48,80},{56,88},{64,... | collective-permute-start | bytes 835592 | tf_op jit(solution)/shard_map/ppermute | solution.py:82
  29.2 18.4 %collective-permute-start.8 = (bf16[64,2176]{1,0:T(8,128)(2,1)S(1)}, bf16[64,2176]{1,0:T(8,128)(2,1)S(1)}, u32[]{:S(2)}, u32[]{:S(2)}) collective-permute-start(bf16[64,2176]{1,0:T(8,128)(2,1)S(1)} %collective-permute-done.6.refs_4_), channel_id=1, source_target_pairs={{0,224},{8,232},{16,240},{24,248},{32,0},{40,8},{48,16},{56,24},{6... | collective-permute-start | bytes 835592 | tf_op jit(solution)/shard_map/ppermute | solution.py:82
  29.9 17.6 %collective-permute-start.10 = (bf16[32,2176]{1,0:T(8,128)(2,1)S(1)}, bf16[32,2176]{1,0:T(8,128)(2,1)S(1)}, u32[]{:S(2)}, u32[]{:S(2)}) collective-permute-start(bf16[32,2176]{1,0:T(8,128)(2,1)S(1)} %slice.79), channel_id=1, source_target_pairs={{0,192},{8,200},{16,208},{24,216},{32,224},{40,232},{48,240},{56,2... | collective-permute-start | bytes 417800 | tf_op jit(solution)/shard_map/ppermute | solution.py:82
  34.1 13.5 %collective-permute-start.9 = (bf16[32,2176]{1,0:T(8,128)(2,1)S(1)}, bf16[32,2176]{1,0:T(8,128)(2,1)S(1)}, u32[]{:S(2)}, u32[]{:S(2)}) collective-permute-start(bf16[32,2176]{1,0:T(8,128)(2,1)S(1)} %slice.78), channel_id=1, source_target_pairs={{0,64},{8,72},{16,80},{24,88},{32,96},{40,104},{48,112},{56,120},{... | collective-permute-start | bytes 417800 | tf_op jit(solution)/shard_map/ppermute | solution.py:82
  34.2 14.7 %copy-start.1 = (bf16[1024,2048]{1,0:T(8,128)(2,1)S(1)}, bf16[1024,2048]{1,0:T(8,128)(2,1)}, u32[]{:S(2)}) copy-start(bf16[1024,2048]{1,0:T(8,128)(2,1)} %window.1) | copy-start | bytes 12582916
  51.8 12.3 %collective-permute-start.17 = (f32[4,128,512]{2,1,0:T(8,128)S(1)}, f32[4,128,512]{2,1,0:T(8,128)S(1)}, u32[]{:S(2)}, u32[]{:S(2)}) collective-permute-start(f32[4,128,512]{2,1,0:T(8,128)S(1)} %get-tuple-element.29), channel_id=1, source_target_pairs={{0,1},{1,0},{2,3},{3,2},{4,5},{5,4},{6,7},{7,6},{8,9},{9,8},{10,11... | collective-permute-start | bytes 3145736 | tf_op jit(solution)/shard_map/ppermute | solution.py:373
  53.6 2.1 %collective-permute-start.11 = (f32[2,320,128]{2,1,0:T(8,128)S(1)}, f32[2,320,128]{2,1,0:T(8,128)S(1)}, u32[]{:S(2)}, u32[]{:S(2)}) collective-permute-start(f32[2,320,128]{2,1,0:T(8,128)S(1)} %get-tuple-element.21), channel_id=1, source_target_pairs={{0,1},{1,0},{2,3},{3,2},{4,5},{5,4},{6,7},{7,6},{8,9},{9,8},{10,11... | collective-permute-start | bytes 983048 | tf_op jit(solution)/shard_map/ppermute | solution.py:373
  55.7 5.5 %collective-permute-start.12 = (f32[320,128]{1,0:T(8,128)S(1)}, f32[320,128]{1,0:T(8,128)S(1)}, u32[]{:S(2)}, u32[]{:S(2)}) collective-permute-start(f32[320,128]{1,0:T(8,128)S(1)} %get-tuple-element.35), channel_id=1, source_target_pairs={{0,2},{1,3},{2,0},{3,1},{4,6},{5,7},{6,4},{7,5},{8,10},{9,11},{10,... | collective-permute-start | bytes 491528 | tf_op jit(solution)/shard_map/ppermute | solution.py:382
  57.1 6.9 %collective-permute-start.14 = (f32[320,128]{1,0:T(8,128)S(1)}, f32[320,128]{1,0:T(8,128)S(1)}, u32[]{:S(2)}, u32[]{:S(2)}) collective-permute-start(f32[320,128]{1,0:T(8,128)S(1)} %get-tuple-element.36), channel_id=1, source_target_pairs={{0,6},{1,7},{2,4},{3,5},{4,2},{5,3},{6,0},{7,1},{8,14},{9,15},{10,... | collective-permute-start | bytes 491528 | tf_op jit(solution)/shard_map/ppermute | solution.py:382
  61.2 7.7 %collective-permute-start.13 = (f32[320,128]{1,0:T(8,128)S(1)}, f32[320,128]{1,0:T(8,128)S(1)}, u32[]{:S(2)}, u32[]{:S(2)}) collective-permute-start(f32[320,128]{1,0:T(8,128)S(1)} %add.96), channel_id=1, source_target_pairs={{0,6},{1,7},{2,4},{3,5},{4,2},{5,3},{6,0},{7,1},{8,14},{9,15},{10,... | collective-permute-start | bytes 491528 | tf_op jit(solution)/shard_map/ppermute | solution.py:383
  64.0 4.9 %collective-permute-start.15 = (f32[320,128]{1,0:T(8,128)S(1)}, f32[320,128]{1,0:T(8,128)S(1)}, u32[]{:S(2)}, u32[]{:S(2)}) collective-permute-start(f32[320,128]{1,0:T(8,128)S(1)} %add.100), channel_id=1, source_target_pairs={{0,2},{1,3},{2,0},{3,1},{4,6},{5,7},{6,4},{7,5},{8,10},{9,11},{10,... | collective-permute-start | bytes 491528 | tf_op jit(solution)/shard_map/ppermute | solution.py:383
  64.3 8.5 %collective-permute-start.18 = (f32[128,512]{1,0:T(8,128)S(1)}, f32[128,512]{1,0:T(8,128)S(1)}, u32[]{:S(2)}, u32[]{:S(2)}) collective-permute-start(f32[128,512]{1,0:T(8,128)S(1)} %get-tuple-element.34), channel_id=1, source_target_pairs={{0,2},{1,3},{2,4},{3,5},{4,6},{5,7},{6,0},{7,1},{8,10},{9,11},{10,... | collective-permute-start | bytes 786440 | tf_op jit(solution)/shard_map/ppermute | solution.py:374
  65.8 14.8 %collective-permute-start.19 = (f32[128,512]{1,0:T(8,128)S(1)}, f32[128,512]{1,0:T(8,128)S(1)}, u32[]{:S(2)}, u32[]{:S(2)}) collective-permute-start(f32[128,512]{1,0:T(8,128)S(1)} %get-tuple-element.32), channel_id=1, source_target_pairs={{0,4},{1,5},{2,6},{3,7},{4,0},{5,1},{6,2},{7,3},{8,12},{9,13},{10,... | collective-permute-start | bytes 786440 | tf_op jit(solution)/shard_map/ppermute | solution.py:374
  66.9 13.7 %collective-permute-start.20 = (f32[128,512]{1,0:T(8,128)S(1)}, f32[128,512]{1,0:T(8,128)S(1)}, u32[]{:S(2)}, u32[]{:S(2)}) collective-permute-start(f32[128,512]{1,0:T(8,128)S(1)} %get-tuple-element.33), channel_id=1, source_target_pairs={{0,6},{1,7},{2,0},{3,1},{4,2},{5,3},{6,4},{7,5},{8,14},{9,15},{10,... | collective-permute-start | bytes 786440 | tf_op jit(solution)/shard_map/ppermute | solution.py:374
  80.8 6.5 %collective-permute-start.21 = (f32[128,512]{1,0:T(8,128)S(1)}, f32[128,512]{1,0:T(8,128)S(1)}, u32[]{:S(2)}, u32[]{:S(2)}) collective-permute-start(f32[128,512]{1,0:T(8,128)S(1)} %fusion.5), channel_id=1, source_target_pairs={{0,2},{1,3},{2,4},{3,5},{4,6},{5,7},{6,0},{7,1},{8,10},{9,11},{10,... | collective-permute-start | bytes 786440 | tf_op jit(solution)/shard_map/ppermute | solution.py:374
  81.3 13.0 %collective-permute-start.22 = (f32[128,512]{1,0:T(8,128)S(1)}, f32[128,512]{1,0:T(8,128)S(1)}, u32[]{:S(2)}, u32[]{:S(2)}) collective-permute-start(f32[128,512]{1,0:T(8,128)S(1)} %fusion.5), channel_id=1, source_target_pairs={{0,4},{1,5},{2,6},{3,7},{4,0},{5,1},{6,2},{7,3},{8,12},{9,13},{10,... | collective-permute-start | bytes 786440 | tf_op jit(solution)/shard_map/ppermute | solution.py:374
  83.7 11.7 %collective-permute-start.23 = (f32[128,512]{1,0:T(8,128)S(1)}, f32[128,512]{1,0:T(8,128)S(1)}, u32[]{:S(2)}, u32[]{:S(2)}) collective-permute-start(f32[128,512]{1,0:T(8,128)S(1)} %fusion.5), channel_id=1, source_target_pairs={{0,6},{1,7},{2,0},{3,1},{4,2},{5,3},{6,4},{7,5},{8,14},{9,15},{10,... | collective-permute-start | bytes 786440 | tf_op jit(solution)/shard_map/ppermute | solution.py:374
  83.8 13.6 %collective-permute-start.16 = (f32[2,320,128]{2,1,0:T(8,128)S(1)}, f32[2,320,128]{2,1,0:T(8,128)S(1)}, u32[]{:S(2)}, u32[]{:S(2)}) collective-permute-start(f32[2,320,128]{2,1,0:T(8,128)S(1)} %pad_maximum_fusion.1.near), channel_id=1, source_target_pairs={{0,1},{1,0},{2,3},{3,2},{4,5},{5,4},{6,7},{7,6},{8,9},{9,8},{10,11... | collective-permute-start | bytes 983048 | tf_op jit(solution)/shard_map/ppermute | solution.py:373
  95.4 22.5 %collective-permute-start.24 = (f32[4,128,512]{2,1,0:T(8,128)S(1)}, f32[4,128,512]{2,1,0:T(8,128)S(1)}, u32[]{:S(2)}, u32[]{:S(2)}) collective-permute-start(f32[4,128,512]{2,1,0:T(8,128)S(1)} %pad_maximum_fusion.near), channel_id=1, source_target_pairs={{0,1},{1,0},{2,3},{3,2},{4,5},{5,4},{6,7},{7,6},{8,9},{9,8},{10,11... | collective-permute-start | bytes 3145736 | tf_op jit(solution)/shard_map/ppermute | solution.py:373
  107.5 10.5 %copy-start = (bf16[1024,64]{0,1:T(8,128)(2,1)S(1)}, bf16[1024,64]{0,1:T(8,128)(2,1)}, u32[]{:S(2)}) copy-start(bf16[1024,64]{0,1:T(8,128)(2,1)} %param.10) | copy-start | bytes 393220

commit v3 on v2

--- a/solution.py
+++ b/solution.py
@@ -68,6 +68,9 @@
     return one(a_low, b_up) + one(a_up, b_low) + one(a_up, b_up)
 
 
+LEFT = 1024
+HELD = LEFT + 128
+PART = 256
 VMEM = pl.BlockSpec(memory_space=pltpu.VMEM)
 
 
@@ -86,41 +89,78 @@
     return [own, up1, down1, up2, down2, up3, down3, up4, down4]
 
 
-def sort_rows(pieces, places, rows, sides):
+def kernel_call(body, out_shape, mib, *args, aliases={}, scratch=()):
+    return pl.pallas_call(
+        body,
+        out_shape=out_shape,
+        in_specs=[VMEM] * len(args),
+        out_specs=jax.tree.map(lambda a: VMEM, out_shape),
+        input_output_aliases=aliases,
+        scratch_shapes=scratch,
+        compiler_params=grant(mib),
+        cost_estimate=pl.CostEstimate(flops=10**6, bytes_accessed=1 << 20, transcendentals=0),
+    )(*args)
+
+
+def prepare_kernel(factor_rows, sides, held, right):
+    held[:, :LEFT] = factor_rows[:, :LEFT]
+    held[:, LEFT:] = jnp.concatenate([sides[...], jnp.zeros_like(sides)], axis=1)
+    for i in range(4):
+        right[16 * i : 16 * i + 16] = factor_rows[:, LEFT + PART * i : LEFT + PART * i + PART]
+
+
+def pack_kernel(near0, near1, near2, near3, right, out):
+    for i, piece in enumerate((near0, near1, near2, near3)):
+        out[16 * i : 16 * i + 16, :HELD] = piece[...]
+    out[:, HELD:] = right[...]
+
+
+def take_kernel(*refs):
+    at = 0
+    for piece in refs[:-1]:
+        size = piece.shape[0]
+        refs[-1][at : at + size] = piece[:, HELD:]
+        at += size
+
+
+def row_of(z, x):
+    return pl.ds(pl.multiple_of((lax.rem(z + NZ, NZ) * NX + lax.rem(x + NX, NX)) * 16, 16), 16)
+
+
+def sort_left(pieces, places, rows, sides):
     z, x, _, _ = place()
     for piece, (turn, first) in zip(pieces, places):
 
         @pl.loop(0, piece.shape[0] // 16)
         def _(i):
-            at = (lax.rem(z + turn + NZ, NZ) * NX + lax.rem(x - first - i + NX, NX)) * 16
-            at = pl.ds(pl.multiple_of(at, 16), 16)
+            at = row_of(z + turn, x - first - i)
             held = piece[pl.ds(pl.multiple_of(16 * i, 16), 16)]
-            rows[at] = held[:, :2048]
-            sides[at] = held[:, 2048:]
+            rows[at, :LEFT] = held[:, :LEFT]
+            sides[at] = held[:, LEFT:HELD]
+
+
+def sort_right(pieces, turns, rows):
+    z, x, _, _ = place()
+    for k, piece in enumerate(pieces):
+        for n, turn in enumerate(turns):
+            for q in range(4):
+                first = 64 * n + 16 * q
+                rows[row_of(z + turn, x - k), LEFT + PART * q : LEFT + PART * q + PART] = piece[first : first + 16]
 
 
 SORTED = (jax.ShapeDtypeStruct((COUNT, 2048), BF16), jax.ShapeDtypeStruct((COUNT, 128), BF16))
 
 
 def early_kernel(*refs):
-    sort_rows(refs[:5], PIECES[:5], *refs[5:])
-
-
-def early(pieces):
-    return pl.pallas_call(
-        early_kernel,
-        name="early",
-        out_shape=SORTED,
-        in_specs=[VMEM] * 5,
-        out_specs=(VMEM, VMEM),
-        compiler_params=grant(4),
-        cost_estimate=pl.CostEstimate(flops=10**6, bytes_accessed=2 << 20, transcendentals=0),
-    )(*pieces)
-
-
-def gram_kernel(rows_in, sides_in, up3, down3, up4, down4, rows, sides, other, mine, blocks):
+    sort_left(refs[:5], PIECES[:5], *refs[5:])
+
+
+def gram_kernel(*refs):
+    pieces, first, second, (rows, sides, other, mine, blocks) = refs[2:6], refs[6:10], refs[10:14], refs[14:]
     _, _, _, c = place()
-    sort_rows((up3, down3, up4, down4), PIECES[5:], rows, sides)
+    sort_left(pieces, PIECES[5:], rows, sides)
+    sort_right(first, (0, -1, 1, -2, 2), rows)
+    sort_right(second, (-3, 3, 4), rows)
     for half in range(2):
         part = lax.dot_general(
             rows[256 * half :], rows[256 * half : 256 * half + 256], (NT, ((), ())), preferred_element_type=F32
@@ -136,19 +176,10 @@
                 out[n, 32 * b : 32 * b + 32] = blocks[b, pl.ds(first, 32), :]
 
 
-def gram(rows, sides, pieces):
+def gram(*args):
     chunk = jax.ShapeDtypeStruct((2, 32 * len(BLOCKS), 128), F32)
-    return pl.pallas_call(
-        gram_kernel,
-        name="gram",
-        out_shape=(*SORTED, chunk, chunk),
-        in_specs=[VMEM] * 6,
-        out_specs=(VMEM,) * 4,
-        input_output_aliases={0: 0, 1: 1},
-        scratch_shapes=[pltpu.VMEM((len(BLOCKS), 128, 128), F32)],
-        compiler_params=grant(10),
-        cost_estimate=pl.CostEstimate(flops=2 * COUNT * COUNT * 2048, bytes_accessed=2 << 20, transcendentals=0),
-    )(rows, sides, *pieces)
+    scratch = [pltpu.VMEM((len(BLOCKS), 128, 128), F32)]
+    return kernel_call(gram_kernel, (*SORTED, chunk, chunk), 10, *args, aliases={0: 0, 1: 1}, scratch=scratch)
 
 
 def schur_kernel(window, rows, other, mine, held, sem):
@@ -373,10 +404,20 @@
     swap = lambda a: lax.ppermute(a, "layer", SWAP)
     along = lambda a, k: lax.ppermute(a, "layer", shift_y(k))
 
-    held = jnp.concatenate([pivot_factor, pivot_sides, jnp.zeros_like(pivot_sides)], axis=1)
-    near = [held] + [lax.ppermute(held, "row", shift_x(k)) for k in (1, 2, 3)]
-    pieces = tower(jnp.concatenate(near, axis=0))
-    rows, sides, gram_other, gram_mine = gram(*early(pieces[:5]), pieces[5:])
+    over_x = lambda a: [a] + [lax.ppermute(a, "row", shift_x(k)) for k in (1, 2, 3)]
+    take = lambda pieces: kernel_call(
+        take_kernel, jax.ShapeDtypeStruct((sum(a.shape[0] for a in pieces), PART), BF16), 2, *pieces
+    )
+
+    shapes = (jax.ShapeDtypeStruct((16, HELD), BF16), jax.ShapeDtypeStruct((64, PART), BF16))
+    held, right = kernel_call(prepare_kernel, shapes, 1, pivot_factor, pivot_sides)
+    packed = jax.ShapeDtypeStruct((64, HELD + PART), BF16)
+    pieces = tower(kernel_call(pack_kernel, packed, 2, *over_x(held), right))
+    first = over_x(take(pieces[:5]))
+    sorted_rows = kernel_call(early_kernel, SORTED, 4, *pieces[:5])
+    second = over_x(take(pieces[5:]))
+    rows, sides, gram_other, gram_mine = gram(*sorted_rows, *pieces[5:], *first, *second)
+
     gram_far = swap(gram_other)
     sums = [gram_mine[n] + gram_far[n] for n in range(2)]
     sums = [sums[n] + lax.ppermute(sums[n], "layer", PAIRS[n]) for n in range(2)]

time: 120 us -> 124 us (1.033)
  starting transfers between devices: 41.5 us -> 55.2 us
  waiting for transfers between devices: 46.8 us -> 36.5 us
    ppermute x8, waiting for transfers between devices: 21 us -> 6.37 us  [tower(): hop = lambda a, k: lax.ppermute(a, 'row', shift_z(k))]
    ppermute x3 -> x9, starting transfers between devices: 5.64 us -> 14 us  [shards(): lax.ppermute(a, 'row', shift_x(k))]
    ppermute x4, starting transfers between devices: 6.02 us -> 11.4 us  [shards(): swap = lambda a: lax.ppermute(a, 'layer', SWAP)]
    ppermute x3 -> x9, waiting for transfers between devices: 2.3 us -> 6.84 us  [shards(): lax.ppermute(a, 'row', shift_x(k))]
    unnamed x4 -> x8, local copies, waits for them, and re-layouts: 0.01 us -> 1.53 us
  transfers between devices with their start and end apart: 25 -> 31, of which waited for: 14 -> 15; matrix products, arithmetic and copies ran while one was open for 2% -> 2% of each run, Pallas kernels for 17% -> 17%
where the time goes in v3:
time: 124 us
  starting transfers between devices  55.2 us (45%)
  waiting for transfers between devices  36.5 us (29%)
  Pallas kernels  26.7 us (22%)
  other arithmetic  2.84 us (2%)
  local copies, waits for them, and re-layouts  1.55 us (1%)
    ppermute x6, waiting for transfers between devices, shards(): along = lambda a, k: lax.ppermute(a, 'layer', shift_y(k))  20 us
    ppermute x8, starting transfers between devices, tower(): hop = lambda a, k: lax.ppermute(a, 'row', shift_z(k))  15.9 us
    ppermute x9, starting transfers between devices, shards(): lax.ppermute(a, 'row', shift_x(k))  14 us
    ppermute x4, starting transfers between devices, shards(): swap = lambda a: lax.ppermute(a, 'layer', SWAP)  11.4 us
    pallas_call x1, Pallas kernels, weigh(): pl.pallas_call(weights_kernel, name='weigh', out_shape=(square, square, j...  10.4 us
    pallas_call x1, Pallas kernels, factor(): pl.pallas_call(factor_kernel, name='factor', out_shape=(square, square),...  10.1 us
    ppermute x6, starting transfers between devices, shards(): along = lambda a, k: lax.ppermute(a, 'layer', shift_y(k))  7.62 us
    ppermute x9, waiting for transfers between devices, shards(): lax.ppermute(a, 'row', shift_x(k))  6.84 us
  transfers between devices with their start and end apart: 31, of which 15 were waited for; matrix products, arithmetic and copies ran while one was open for 2% of the time, Pallas kernels for 17%

profile of v3, /device:TPU:1, one launch (start us, length us, event | category | flops | bytes accessed | tf_op | source)
XLA Modules:
  0.0 123.7 jit_solution(17527177725443881803)
XLA Ops:
  0.6 0.8 copy-done.1
  1.5 0.7 copy-done.2
  2.2 2.0 %collective-permute-start = (bf16[16,1152]{1,0:T(8,128)(2,1)S(1)}, bf16[16,1152]{1,0:T(8,128)(2,1)S(1)}, u32[]{:S(2)}, u32[]{:S(2)}) collective-permute-start(bf16[16,1152]{1,0:T(8,128)(2,1)S(1)} %get-tuple-element.20.near0), channel_id=1, source_target_pairs={{0,8},{8,16},{16,24},{24,0},{32,40},{40,48},{48,56},{56,32},{64,72... | collective-permute-start | bytes 110600 | tf_op jit(solution)/shard_map/ppermute | solution.py:407
  4.2 2.5 %collective-permute-start.1 = (bf16[16,1152]{1,0:T(8,128)(2,1)S(1)}, bf16[16,1152]{1,0:T(8,128)(2,1)S(1)}, u32[]{:S(2)}, u32[]{:S(2)}) collective-permute-start(bf16[16,1152]{1,0:T(8,128)(2,1)S(1)} %get-tuple-element.20.near0), channel_id=1, source_target_pairs={{0,16},{8,24},{16,0},{24,8},{32,48},{40,56},{48,32},{56,40},{64,80... | collective-permute-start | bytes 110600 | tf_op jit(solution)/shard_map/ppermute | solution.py:407
  6.6 1.2 collective-permute-start.2
  7.8 0.7 collective-permute-done.1.near2
  8.5 1.2 %collective-permute-done.2.near3 = bf16[16,1152]{1,0:T(8,128)(2,1)S(1)} collective-permute-done((bf16[16,1152]{1,0:T(8,128)(2,1)S(1)}, bf16[16,1152]{1,0:T(8,128)(2,1)S(1)}, u32[]{:S(2)}, u32[]{:S(2)}) %collective-permute-start.2) | collective-permute-done | bytes 36896 | tf_op jit(solution)/shard_map/ppermute | solution.py:407
  9.8 3.1 %collective-permute-start.5 = (bf16[64,1408]{1,0:T(8,128)(2,1)S(1)}, bf16[64,1408]{1,0:T(8,128)(2,1)S(1)}, u32[]{:S(2)}, u32[]{:S(2)}) collective-permute-start(bf16[64,1408]{1,0:T(8,128)(2,1)S(1)} %shard_map.78.refs_0_), channel_id=1, source_target_pairs={{0,64},{8,72},{16,80},{24,88},{32,96},{40,104},{48,112},{56,120},{... | collective-permute-start | bytes 540680 | tf_op jit(solution)/shard_map/ppermute | solution.py:85
  12.8 3.1 %collective-permute-start.6 = (bf16[64,1408]{1,0:T(8,128)(2,1)S(1)}, bf16[64,1408]{1,0:T(8,128)(2,1)S(1)}, u32[]{:S(2)}, u32[]{:S(2)}) collective-permute-start(bf16[64,1408]{1,0:T(8,128)(2,1)S(1)} %shard_map.78.refs_0_), channel_id=1, source_target_pairs={{0,192},{8,200},{16,208},{24,216},{32,224},{40,232},{48,240},{56,2... | collective-permute-start | bytes 540680 | tf_op jit(solution)/shard_map/ppermute | solution.py:85
  16.0 0.7 collective-permute-start.3
  16.7 1.9 %collective-permute-start.4 = (bf16[64,1408]{1,0:T(8,128)(2,1)S(1)}, bf16[64,1408]{1,0:T(8,128)(2,1)S(1)}, u32[]{:S(2)}, u32[]{:S(2)}) collective-permute-start(bf16[64,1408]{1,0:T(8,128)(2,1)S(1)} %shard_map.78.refs_0_), channel_id=1, source_target_pairs={{0,224},{8,232},{16,240},{24,248},{32,0},{40,8},{48,16},{56,24},{6... | collective-permute-start | bytes 540680 | tf_op jit(solution)/shard_map/ppermute | solution.py:85
  18.6 1.2 %collective-permute-done.5.refs_3_ = bf16[64,1408]{1,0:T(8,128)(2,1)S(1)} collective-permute-done((bf16[64,1408]{1,0:T(8,128)(2,1)S(1)}, bf16[64,1408]{1,0:T(8,128)(2,1)S(1)}, u32[]{:S(2)}, u32[]{:S(2)}) %collective-permute-start.5) | collective-permute-done | bytes 180256 | tf_op jit(solution)/shard_map/ppermute | solution.py:85
  19.9 4.5 %collective-permute-start.7 = (bf16[64,1408]{1,0:T(8,128)(2,1)S(1)}, bf16[64,1408]{1,0:T(8,128)(2,1)S(1)}, u32[]{:S(2)}, u32[]{:S(2)}) collective-permute-start(bf16[64,1408]{1,0:T(8,128)(2,1)S(1)} %collective-permute-done.5.refs_3_), channel_id=1, source_target_pairs={{0,32},{8,40},{16,48},{24,56},{32,64},{40,72},{48,80},{56,88},{64,... | collective-permute-start | bytes 540680 | tf_op jit(solution)/shard_map/ppermute | solution.py:85
  24.4 0.2 collective-permute-done.6.refs_4_
  24.6 0.0 collective-permute-start.8
  24.7 3.0 %collective-permute-done.3.refs_1_ = bf16[64,1408]{1,0:T(8,128)(2,1)S(1)} collective-permute-done((bf16[64,1408]{1,0:T(8,128)(2,1)S(1)}, bf16[64,1408]{1,0:T(8,128)(2,1)S(1)}, u32[]{:S(2)}, u32[]{:S(2)}) %collective-permute-start.3) | collective-permute-done | bytes 180256 | tf_op jit(solution)/shard_map/ppermute | solution.py:85
  27.7 0.1 collective-permute-start.11
  27.8 2.4 %collective-permute-start.10 = (bf16[32,1408]{1,0:T(8,128)(2,1)S(1)}, bf16[32,1408]{1,0:T(8,128)(2,1)S(1)}, u32[]{:S(2)}, u32[]{:S(2)}) collective-permute-start(bf16[32,1408]{1,0:T(8,128)(2,1)S(1)} %slice.79), channel_id=1, source_target_pairs={{0,192},{8,200},{16,208},{24,216},{32,224},{40,232},{48,240},{56,2... | collective-permute-start | bytes 270344 | tf_op jit(solution)/shard_map/ppermute | solution.py:85
  30.2 0.1 collective-permute-start.9
  30.3 0.7 convert_element_type.4
  31.0 1.9 %collective-permute-done.10.refs_3_.refs_5_ = bf16[32,1408]{1,0:T(8,128)(2,1)S(1)} collective-permute-done((bf16[32,1408]{1,0:T(8,128)(2,1)S(1)}, bf16[32,1408]{1,0:T(8,128)(2,1)S(1)}, u32[]{:S(2)}, u32[]{:S(2)}) %collective-permute-start.10) | collective-permute-done | bytes 90144 | tf_op jit(solution)/shard_map/ppermute | solution.py:85
  32.9 3.2 %collective-permute-start.12 = (bf16[320,256]{1,0:T(8,128)(2,1)S(1)}, bf16[320,256]{1,0:T(8,128)(2,1)S(1)}, u32[]{:S(2)}, u32[]{:S(2)}) collective-permute-start(bf16[320,256]{1,0:T(8,128)(2,1)S(1)} %shard_map.80.refs_6_), channel_id=1, source_target_pairs={{0,16},{8,24},{16,0},{24,8},{32,48},{40,56},{48,32},{56,40},{64,80... | collective-permute-start | bytes 491528 | tf_op jit(solution)/shard_map/ppermute | solution.py:407
  36.1 0.0 collective-permute-done.9.refs_2_.refs_4_
  36.1 2.4 %collective-permute-start.13 = (bf16[320,256]{1,0:T(8,128)(2,1)S(1)}, bf16[320,256]{1,0:T(8,128)(2,1)S(1)}, u32[]{:S(2)}, u32[]{:S(2)}) collective-permute-start(bf16[320,256]{1,0:T(8,128)(2,1)S(1)} %shard_map.80.refs_6_), channel_id=1, source_target_pairs={{0,24},{8,0},{16,8},{24,16},{32,56},{40,32},{48,40},{56,48},{64,88... | collective-permute-start | bytes 491528 | tf_op jit(solution)/shard_map/ppermute | solution.py:407
  38.4 0.0 collective-permute-done.7.refs_0_.refs_2_
  38.5 0.1 collective-permute-start.14
  38.6 1.7 %collective-permute-start.15 = (bf16[192,256]{1,0:T(8,128)(2,1)S(1)}, bf16[192,256]{1,0:T(8,128)(2,1)S(1)}, u32[]{:S(2)}, u32[]{:S(2)}) collective-permute-start(bf16[192,256]{1,0:T(8,128)(2,1)S(1)} %shard_map.81.refs_10_), channel_id=1, source_target_pairs={{0,16},{8,24},{16,0},{24,8},{32,48},{40,56},{48,32},{56,40},{64,80... | collective-permute-start | bytes 294920 | tf_op jit(solution)/shard_map/ppermute | solution.py:407
  40.3 1.0 collective-permute-start.16
  41.2 0.2 shard_map.79
  41.5 4.5 %collective-permute-done.14.refs_11_ = bf16[192,256]{1,0:T(8,128)(2,1)S(1)} collective-permute-done((bf16[192,256]{1,0:T(8,128)(2,1)S(1)}, bf16[192,256]{1,0:T(8,128)(2,1)S(1)}, u32[]{:S(2)}, u32[]{:S(2)}) %collective-permute-start.14) | collective-permute-done | bytes 98336 | tf_op jit(solution)/shard_map/ppermute | solution.py:407
  46.0 0.3 collective-permute-done.16.refs_13_
  46.4 1.3 %shard_map.82 = (bf16[512,2048]{1,0:T(8,128)(2,1)S(1)}, bf16[512,128]{1,0:T(8,128)(2,1)S(1)}, f32[2,320,128]{2,1,0:T(8,128)S(1)}, f32[2,320,128]{2,1,0:T(8,128)S(1)}) custom-call(bf16[512,2048]{1,0:T(8,128)(2,1)S(1)} %get-tuple-element.22.refs_0_, bf16[512,128]{1,0:T(8,128)(2,1)S(1)} %get-tuple-element.23.refs_1_, ...), custom_call_target="tpu_custom_call", output_to_operand_aliasing={{0}: (0, {}), {1}: (1, {})} | custom-call | flops 1000000 | bytes 1048576 | tf_op jit(solution)/shard_map/pallas_call | solution.py:93
  47.7 2.9 %schur.1 = (f32[4,128,512]{2,1,0:T(8,128)S(1)}, f32[4,128,512]{2,1,0:T(8,128)S(1)}) custom-call(bf16[1024,2048]{1,0:T(8,128)(2,1)S(1)} %copy-done.3, bf16[512,2048]{1,0:T(8,128)(2,1)S(1)} %get-tuple-element.31.rows), custom_call_target="tpu_custom_call" | custom-call | flops 2147483648 | bytes 8388608 | tf_op jit(solution)/shard_map/schur/pallas_call | solution.py:211
  50.6 6.5 %collective-permute-start.23 = (f32[4,128,512]{2,1,0:T(8,128)S(1)}, f32[4,128,512]{2,1,0:T(8,128)S(1)}, u32[]{:S(2)}, u32[]{:S(2)}) collective-permute-start(f32[4,128,512]{2,1,0:T(8,128)S(1)} %get-tuple-element.33), channel_id=1, source_target_pairs={{0,1},{1,0},{2,3},{3,2},{4,5},{5,4},{6,7},{7,6},{8,9},{9,8},{10,11... | collective-permute-start | bytes 3145736 | tf_op jit(solution)/shard_map/ppermute | solution.py:404
  57.1 0.7 dynamic-slice_convert_fusion
  57.8 0.0 collective-permute-start.17
  57.8 0.7 select_add_fusion.cov
  58.6 1.3 %collective-permute-done.17 = f32[2,320,128]{2,1,0:T(8,128)S(1)} collective-permute-done((f32[2,320,128]{2,1,0:T(8,128)S(1)}, f32[2,320,128]{2,1,0:T(8,128)S(1)}, u32[]{:S(2)}, u32[]{:S(2)}) %collective-permute-start.17) | collective-permute-done | bytes 327712 | tf_op jit(solution)/shard_map/ppermute | solution.py:404
  59.9 1.4 %collective-permute-start.18 = (f32[320,128]{1,0:T(8,128)S(1)}, f32[320,128]{1,0:T(8,128)S(1)}, u32[]{:S(2)}, u32[]{:S(2)}) collective-permute-start(f32[320,128]{1,0:T(8,128)S(1)} %get-tuple-element.39), channel_id=1, source_target_pairs={{0,2},{1,3},{2,0},{3,1},{4,6},{5,7},{6,4},{7,5},{8,10},{9,11},{10,... | collective-permute-start | bytes 491528 | tf_op jit(solution)/shard_map/ppermute | solution.py:423
  61.3 1.9 %collective-permute-start.20 = (f32[320,128]{1,0:T(8,128)S(1)}, f32[320,128]{1,0:T(8,128)S(1)}, u32[]{:S(2)}, u32[]{:S(2)}) collective-permute-start(f32[320,128]{1,0:T(8,128)S(1)} %get-tuple-element.40), channel_id=1, source_target_pairs={{0,6},{1,7},{2,4},{3,5},{4,2},{5,3},{6,0},{7,1},{8,14},{9,15},{10,... | collective-permute-start | bytes 491528 | tf_op jit(solution)/shard_map/ppermute | solution.py:423
  63.2 0.2 exponential_multiply_fusion
  63.4 1.9 %collective-permute-done.18 = f32[320,128]{1,0:T(8,128)S(1)} collective-permute-done((f32[320,128]{1,0:T(8,128)S(1)}, f32[320,128]{1,0:T(8,128)S(1)}, u32[]{:S(2)}, u32[]{:S(2)}) %collective-permute-start.18) | collective-permute-done | bytes 163872 | tf_op jit(solution)/shard_map/ppermute | solution.py:423
  65.4 2.8 %collective-permute-start.19 = (f32[320,128]{1,0:T(8,128)S(1)}, f32[320,128]{1,0:T(8,128)S(1)}, u32[]{:S(2)}, u32[]{:S(2)}) collective-permute-start(f32[320,128]{1,0:T(8,128)S(1)} %add.96), channel_id=1, source_target_pairs={{0,6},{1,7},{2,4},{3,5},{4,2},{5,3},{6,0},{7,1},{8,14},{9,15},{10,... | collective-permute-start | bytes 491528 | tf_op jit(solution)/shard_map/ppermute | solution.py:424
  68.3 0.1 collective-permute-start.21
  68.4 0.1 fusion.1
  68.5 1.5 %collective-permute-start.24 = (f32[128,512]{1,0:T(8,128)S(1)}, f32[128,512]{1,0:T(8,128)S(1)}, u32[]{:S(2)}, u32[]{:S(2)}) collective-permute-start(f32[128,512]{1,0:T(8,128)S(1)} %get-tuple-element.38), channel_id=1, source_target_pairs={{0,2},{1,3},{2,4},{3,5},{4,6},{5,7},{6,0},{7,1},{8,10},{9,11},{10,... | collective-permute-start | bytes 786440 | tf_op jit(solution)/shard_map/ppermute | solution.py:405
  70.0 1.1 collective-permute-start.25
  71.1 2.0 %collective-permute-start.26 = (f32[128,512]{1,0:T(8,128)S(1)}, f32[128,512]{1,0:T(8,128)S(1)}, u32[]{:S(2)}, u32[]{:S(2)}) collective-permute-start(f32[128,512]{1,0:T(8,128)S(1)} %get-tuple-element.37), channel_id=1, source_target_pairs={{0,6},{1,7},{2,0},{3,1},{4,2},{5,3},{6,4},{7,5},{8,14},{9,15},{10,... | collective-permute-start | bytes 786440 | tf_op jit(solution)/shard_map/ppermute | solution.py:405
  73.2 3.8 %collective-permute-done.24 = f32[128,512]{1,0:T(8,128)S(1)} collective-permute-done((f32[128,512]{1,0:T(8,128)S(1)}, f32[128,512]{1,0:T(8,128)S(1)}, u32[]{:S(2)}, u32[]{:S(2)}) %collective-permute-start.24) | collective-permute-done | bytes 262176 | tf_op jit(solution)/shard_map/ppermute | solution.py:405
  77.0 7.8 %collective-permute-done.25 = f32[128,512]{1,0:T(8,128)S(1)} collective-permute-done((f32[128,512]{1,0:T(8,128)S(1)}, f32[128,512]{1,0:T(8,128)S(1)}, u32[]{:S(2)}, u32[]{:S(2)}) %collective-permute-start.25) | collective-permute-done | bytes 262176 | tf_op jit(solution)/shard_map/ppermute | solution.py:405
  84.8 0.2 fusion.5
  85.0 0.5 collective-permute-start.27
  85.5 2.4 %collective-permute-start.28 = (f32[128,512]{1,0:T(8,128)S(1)}, f32[128,512]{1,0:T(8,128)S(1)}, u32[]{:S(2)}, u32[]{:S(2)}) collective-permute-start(f32[128,512]{1,0:T(8,128)S(1)} %fusion.5), channel_id=1, source_target_pairs={{0,4},{1,5},{2,6},{3,7},{4,0},{5,1},{6,2},{7,3},{8,12},{9,13},{10,... | collective-permute-start | bytes 786440 | tf_op jit(solution)/shard_map/ppermute | solution.py:405
  87.9 0.1 collective-permute-start.29
  88.0 3.1 %collective-permute-start.22 = (f32[2,320,128]{2,1,0:T(8,128)S(1)}, f32[2,320,128]{2,1,0:T(8,128)S(1)}, u32[]{:S(2)}, u32[]{:S(2)}) collective-permute-start(f32[2,320,128]{2,1,0:T(8,128)S(1)} %pad_maximum_fusion.1.near), channel_id=1, source_target_pairs={{0,1},{1,0},{2,3},{3,2},{4,5},{5,4},{6,7},{7,6},{8,9},{9,8},{10,11... | collective-permute-start | bytes 983048 | tf_op jit(solution)/shard_map/ppermute | solution.py:404
  91.2 0.3 collective-permute-done.27
  91.5 7.0 %collective-permute-done.28 = f32[128,512]{1,0:T(8,128)S(1)} collective-permute-done((f32[128,512]{1,0:T(8,128)S(1)}, f32[128,512]{1,0:T(8,128)S(1)}, u32[]{:S(2)}, u32[]{:S(2)}) %collective-permute-start.28) | collective-permute-done | bytes 262176 | tf_op jit(solution)/shard_map/ppermute | solution.py:405
  98.5 1.1 collective-permute-done.29
  99.6 0.1 pad_maximum_fusion.near
  99.6 1.8 %collective-permute-start.30 = (f32[4,128,512]{2,1,0:T(8,128)S(1)}, f32[4,128,512]{2,1,0:T(8,128)S(1)}, u32[]{:S(2)}, u32[]{:S(2)}) collective-permute-start(f32[4,128,512]{2,1,0:T(8,128)S(1)} %pad_maximum_fusion.near), channel_id=1, source_target_pairs={{0,1},{1,0},{2,3},{3,2},{4,5},{5,4},{6,7},{7,6},{8,9},{9,8},{10,11... | collective-permute-start | bytes 3145736 | tf_op jit(solution)/shard_map/ppermute | solution.py:404
  101.4 10.1 %factor.1 = (f32[512,512]{1,0:T(8,128)S(1)}, f32[512,512]{1,0:T(8,128)S(1)}) custom-call(f32[512,512]{1,0:T(8,128)S(1)} %select_add_fusion.cov, f32[2,320,128]{2,1,0:T(8,128)S(1)} %pad_maximum_fusion.1.near, f32[2,320,128]{2,1,0:T(8,128)S(1)} %collective-permute-done.22.far), custom_call_target="tpu_custom_call" | custom-call | flops 10000000000 | bytes 4194304 | tf_op jit(solution)/shard_map/factor/pallas_call | solution.py:343
  111.5 0.0 copy-start
  111.5 10.4 %weigh.1 = (f32[512,512]{1,0:T(8,128)S(1)}, f32[512,512]{1,0:T(8,128)S(1)}, f32[128,512]{1,0:T(8,128)S(1)}) custom-call(f32[512,512]{1,0:T(8,128)S(1)} %get-tuple-element.26.a_in, f32[512,512]{1,0:T(8,128)S(1)} %get-tuple-element.27.e_in, bf16[512,128]{1,0:T(8,128)(2,1)S(1)} %get-tuple-element.28.sides), custom_call_target="tpu_custom_call", output_to_operand_aliasing={{0}: (0, {}), {1}: (1, {})} | custom-call | flops 10000000000 | bytes 4194304 | tf_op jit(solution)/shard_map/weigh/pallas_call | solution.py:366
  121.9 1.8 %finish.1 = (f32[64,1024]{1,0:T(8,128)}, f32[64,1024]{1,0:T(8,128)}) custom-call(f32[128,512]{1,0:T(8,128)S(1)} %get-tuple-element.29.weights, f32[4,128,512]{2,1,0:T(8,128)S(1)} %pad_maximum_fusion.near, f32[4,128,512]{2,1,0:T(8,128)S(1)} %collective-permute-done.30.far, bf16[64,1024]{1,0:T(8,128)(2,1)S(1)} %bitcast.33), custom_call_target="tpu_custom_call" | custom-call | flops 402653184 | bytes 3145728 | tf_op jit(solution)/shard_map/finish/pallas_call | solution.py:391
  (33 shorter events, 0.2 us)
Async XLA Ops:
  0.6 0.8 copy-start.1
  1.5 0.7 copy-start.2
  2.2 5.6 %collective-permute-start = (bf16[16,1152]{1,0:T(8,128)(2,1)S(1)}, bf16[16,1152]{1,0:T(8,128)(2,1)S(1)}, u32[]{:S(2)}, u32[]{:S(2)}) collective-permute-start(bf16[16,1152]{1,0:T(8,128)(2,1)S(1)} %get-tuple-element.20.near0), channel_id=1, source_target_pairs={{0,8},{8,16},{16,24},{24,0},{32,40},{40,48},{48,56},{56,32},{64,72... | collective-permute-start | bytes 110600 | tf_op jit(solution)/shard_map/ppermute | solution.py:407
  4.2 4.3 %collective-permute-start.1 = (bf16[16,1152]{1,0:T(8,128)(2,1)S(1)}, bf16[16,1152]{1,0:T(8,128)(2,1)S(1)}, u32[]{:S(2)}, u32[]{:S(2)}) collective-permute-start(bf16[16,1152]{1,0:T(8,128)(2,1)S(1)} %get-tuple-element.20.near0), channel_id=1, source_target_pairs={{0,16},{8,24},{16,0},{24,8},{32,48},{40,56},{48,32},{56,40},{64,80... | collective-permute-start | bytes 110600 | tf_op jit(solution)/shard_map/ppermute | solution.py:407
  6.6 3.1 %collective-permute-start.2 = (bf16[16,1152]{1,0:T(8,128)(2,1)S(1)}, bf16[16,1152]{1,0:T(8,128)(2,1)S(1)}, u32[]{:S(2)}, u32[]{:S(2)}) collective-permute-start(bf16[16,1152]{1,0:T(8,128)(2,1)S(1)} %get-tuple-element.20.near0), channel_id=1, source_target_pairs={{0,24},{8,0},{16,8},{24,16},{32,56},{40,32},{48,40},{56,48},{64,88... | collective-permute-start | bytes 110600 | tf_op jit(solution)/shard_map/ppermute | solution.py:407
  9.8 10.1 %collective-permute-start.5 = (bf16[64,1408]{1,0:T(8,128)(2,1)S(1)}, bf16[64,1408]{1,0:T(8,128)(2,1)S(1)}, u32[]{:S(2)}, u32[]{:S(2)}) collective-permute-start(bf16[64,1408]{1,0:T(8,128)(2,1)S(1)} %shard_map.78.refs_0_), channel_id=1, source_target_pairs={{0,64},{8,72},{16,80},{24,88},{32,96},{40,104},{48,112},{56,120},{... | collective-permute-start | bytes 540680 | tf_op jit(solution)/shard_map/ppermute | solution.py:85
  12.8 11.8 %collective-permute-start.6 = (bf16[64,1408]{1,0:T(8,128)(2,1)S(1)}, bf16[64,1408]{1,0:T(8,128)(2,1)S(1)}, u32[]{:S(2)}, u32[]{:S(2)}) collective-permute-start(bf16[64,1408]{1,0:T(8,128)(2,1)S(1)} %shard_map.78.refs_0_), channel_id=1, source_target_pairs={{0,192},{8,200},{16,208},{24,216},{32,224},{40,232},{48,240},{56,2... | collective-permute-start | bytes 540680 | tf_op jit(solution)/shard_map/ppermute | solution.py:85
  16.0 11.7 %collective-permute-start.3 = (bf16[64,1408]{1,0:T(8,128)(2,1)S(1)}, bf16[64,1408]{1,0:T(8,128)(2,1)S(1)}, u32[]{:S(2)}, u32[]{:S(2)}) collective-permute-start(bf16[64,1408]{1,0:T(8,128)(2,1)S(1)} %shard_map.78.refs_0_), channel_id=1, source_target_pairs={{0,32},{8,40},{16,48},{24,56},{32,64},{40,72},{48,80},{56,88},{64,... | collective-permute-start | bytes 540680 | tf_op jit(solution)/shard_map/ppermute | solution.py:85
  16.7 11.0 %collective-permute-start.4 = (bf16[64,1408]{1,0:T(8,128)(2,1)S(1)}, bf16[64,1408]{1,0:T(8,128)(2,1)S(1)}, u32[]{:S(2)}, u32[]{:S(2)}) collective-permute-start(bf16[64,1408]{1,0:T(8,128)(2,1)S(1)} %shard_map.78.refs_0_), channel_id=1, source_target_pairs={{0,224},{8,232},{16,240},{24,248},{32,0},{40,8},{48,16},{56,24},{6... | collective-permute-start | bytes 540680 | tf_op jit(solution)/shard_map/ppermute | solution.py:85
  19.9 18.6 %collective-permute-start.7 = (bf16[64,1408]{1,0:T(8,128)(2,1)S(1)}, bf16[64,1408]{1,0:T(8,128)(2,1)S(1)}, u32[]{:S(2)}, u32[]{:S(2)}) collective-permute-start(bf16[64,1408]{1,0:T(8,128)(2,1)S(1)} %collective-permute-done.5.refs_3_), channel_id=1, source_target_pairs={{0,32},{8,40},{16,48},{24,56},{32,64},{40,72},{48,80},{56,88},{64,... | collective-permute-start | bytes 540680 | tf_op jit(solution)/shard_map/ppermute | solution.py:85
  24.6 13.8 %collective-permute-start.8 = (bf16[64,1408]{1,0:T(8,128)(2,1)S(1)}, bf16[64,1408]{1,0:T(8,128)(2,1)S(1)}, u32[]{:S(2)}, u32[]{:S(2)}) collective-permute-start(bf16[64,1408]{1,0:T(8,128)(2,1)S(1)} %collective-permute-done.6.refs_4_), channel_id=1, source_target_pairs={{0,224},{8,232},{16,240},{24,248},{32,0},{40,8},{48,16},{56,24},{6... | collective-permute-start | bytes 540680 | tf_op jit(solution)/shard_map/ppermute | solution.py:85
  27.7 12.6 %collective-permute-start.11 = (bf16[320,256]{1,0:T(8,128)(2,1)S(1)}, bf16[320,256]{1,0:T(8,128)(2,1)S(1)}, u32[]{:S(2)}, u32[]{:S(2)}) collective-permute-start(bf16[320,256]{1,0:T(8,128)(2,1)S(1)} %shard_map.80.refs_6_), channel_id=1, source_target_pairs={{0,8},{8,16},{16,24},{24,0},{32,40},{40,48},{48,56},{56,32},{64,72... | collective-permute-start | bytes 491528 | tf_op jit(solution)/shard_map/ppermute | solution.py:407
  27.8 5.1 %collective-permute-start.10 = (bf16[32,1408]{1,0:T(8,128)(2,1)S(1)}, bf16[32,1408]{1,0:T(8,128)(2,1)S(1)}, u32[]{:S(2)}, u32[]{:S(2)}) collective-permute-start(bf16[32,1408]{1,0:T(8,128)(2,1)S(1)} %slice.79), channel_id=1, source_target_pairs={{0,192},{8,200},{16,208},{24,216},{32,224},{40,232},{48,240},{56,2... | collective-permute-start | bytes 270344 | tf_op jit(solution)/shard_map/ppermute | solution.py:85
  30.2 5.9 %collective-permute-start.9 = (bf16[32,1408]{1,0:T(8,128)(2,1)S(1)}, bf16[32,1408]{1,0:T(8,128)(2,1)S(1)}, u32[]{:S(2)}, u32[]{:S(2)}) collective-permute-start(bf16[32,1408]{1,0:T(8,128)(2,1)S(1)} %slice.78), channel_id=1, source_target_pairs={{0,64},{8,72},{16,80},{24,88},{32,96},{40,104},{48,112},{56,120},{... | collective-permute-start | bytes 270344 | tf_op jit(solution)/shard_map/ppermute | solution.py:85
  32.9 8.6 %collective-permute-start.12 = (bf16[320,256]{1,0:T(8,128)(2,1)S(1)}, bf16[320,256]{1,0:T(8,128)(2,1)S(1)}, u32[]{:S(2)}, u32[]{:S(2)}) collective-permute-start(bf16[320,256]{1,0:T(8,128)(2,1)S(1)} %shard_map.80.refs_6_), channel_id=1, source_target_pairs={{0,16},{8,24},{16,0},{24,8},{32,48},{40,56},{48,32},{56,40},{64,80... | collective-permute-start | bytes 491528 | tf_op jit(solution)/shard_map/ppermute | solution.py:407
  36.1 5.4 %collective-permute-start.13 = (bf16[320,256]{1,0:T(8,128)(2,1)S(1)}, bf16[320,256]{1,0:T(8,128)(2,1)S(1)}, u32[]{:S(2)}, u32[]{:S(2)}) collective-permute-start(bf16[320,256]{1,0:T(8,128)(2,1)S(1)} %shard_map.80.refs_6_), channel_id=1, source_target_pairs={{0,24},{8,0},{16,8},{24,16},{32,56},{40,32},{48,40},{56,48},{64,88... | collective-permute-start | bytes 491528 | tf_op jit(solution)/shard_map/ppermute | solution.py:407
  38.5 7.6 %collective-permute-start.14 = (bf16[192,256]{1,0:T(8,128)(2,1)S(1)}, bf16[192,256]{1,0:T(8,128)(2,1)S(1)}, u32[]{:S(2)}, u32[]{:S(2)}) collective-permute-start(bf16[192,256]{1,0:T(8,128)(2,1)S(1)} %shard_map.81.refs_10_), channel_id=1, source_target_pairs={{0,8},{8,16},{16,24},{24,0},{32,40},{40,48},{48,56},{56,32},{64,72... | collective-permute-start | bytes 294920 | tf_op jit(solution)/shard_map/ppermute | solution.py:407
  38.6 7.5 %collective-permute-start.15 = (bf16[192,256]{1,0:T(8,128)(2,1)S(1)}, bf16[192,256]{1,0:T(8,128)(2,1)S(1)}, u32[]{:S(2)}, u32[]{:S(2)}) collective-permute-start(bf16[192,256]{1,0:T(8,128)(2,1)S(1)} %shard_map.81.refs_10_), channel_id=1, source_target_pairs={{0,16},{8,24},{16,0},{24,8},{32,48},{40,56},{48,32},{56,40},{64,80... | collective-permute-start | bytes 294920 | tf_op jit(solution)/shard_map/ppermute | solution.py:407
  40.3 6.1 %collective-permute-start.16 = (bf16[192,256]{1,0:T(8,128)(2,1)S(1)}, bf16[192,256]{1,0:T(8,128)(2,1)S(1)}, u32[]{:S(2)}, u32[]{:S(2)}) collective-permute-start(bf16[192,256]{1,0:T(8,128)(2,1)S(1)} %shard_map.81.refs_10_), channel_id=1, source_target_pairs={{0,24},{8,0},{16,8},{24,16},{32,56},{40,32},{48,40},{56,48},{64,88... | collective-permute-start | bytes 294920 | tf_op jit(solution)/shard_map/ppermute | solution.py:407
  41.2 6.5 %copy-start.3 = (bf16[1024,2048]{1,0:T(8,128)(2,1)S(1)}, bf16[1024,2048]{1,0:T(8,128)(2,1)}, u32[]{:S(2)}) copy-start(bf16[1024,2048]{1,0:T(8,128)(2,1)} %window.1) | copy-start | bytes 12582916
  50.6 17.7 %collective-permute-start.23 = (f32[4,128,512]{2,1,0:T(8,128)S(1)}, f32[4,128,512]{2,1,0:T(8,128)S(1)}, u32[]{:S(2)}, u32[]{:S(2)}) collective-permute-start(f32[4,128,512]{2,1,0:T(8,128)S(1)} %get-tuple-element.33), channel_id=1, source_target_pairs={{0,1},{1,0},{2,3},{3,2},{4,5},{5,4},{6,7},{7,6},{8,9},{9,8},{10,11... | collective-permute-start | bytes 3145736 | tf_op jit(solution)/shard_map/ppermute | solution.py:404
  57.8 2.1 %collective-permute-start.17 = (f32[2,320,128]{2,1,0:T(8,128)S(1)}, f32[2,320,128]{2,1,0:T(8,128)S(1)}, u32[]{:S(2)}, u32[]{:S(2)}) collective-permute-start(f32[2,320,128]{2,1,0:T(8,128)S(1)} %get-tuple-element.25), channel_id=1, source_target_pairs={{0,1},{1,0},{2,3},{3,2},{4,5},{5,4},{6,7},{7,6},{8,9},{9,8},{10,11... | collective-permute-start | bytes 983048 | tf_op jit(solution)/shard_map/ppermute | solution.py:404
  59.9 5.5 %collective-permute-start.18 = (f32[320,128]{1,0:T(8,128)S(1)}, f32[320,128]{1,0:T(8,128)S(1)}, u32[]{:S(2)}, u32[]{:S(2)}) collective-permute-start(f32[320,128]{1,0:T(8,128)S(1)} %get-tuple-element.39), channel_id=1, source_target_pairs={{0,2},{1,3},{2,0},{3,1},{4,6},{5,7},{6,4},{7,5},{8,10},{9,11},{10,... | collective-permute-start | bytes 491528 | tf_op jit(solution)/shard_map/ppermute | solution.py:423
  61.3 6.9 %collective-permute-start.20 = (f32[320,128]{1,0:T(8,128)S(1)}, f32[320,128]{1,0:T(8,128)S(1)}, u32[]{:S(2)}, u32[]{:S(2)}) collective-permute-start(f32[320,128]{1,0:T(8,128)S(1)} %get-tuple-element.40), channel_id=1, source_target_pairs={{0,6},{1,7},{2,4},{3,5},{4,2},{5,3},{6,0},{7,1},{8,14},{9,15},{10,... | collective-permute-start | bytes 491528 | tf_op jit(solution)/shard_map/ppermute | solution.py:423
  65.4 7.7 %collective-permute-start.19 = (f32[320,128]{1,0:T(8,128)S(1)}, f32[320,128]{1,0:T(8,128)S(1)}, u32[]{:S(2)}, u32[]{:S(2)}) collective-permute-start(f32[320,128]{1,0:T(8,128)S(1)} %add.96), channel_id=1, source_target_pairs={{0,6},{1,7},{2,4},{3,5},{4,2},{5,3},{6,0},{7,1},{8,14},{9,15},{10,... | collective-permute-start | bytes 491528 | tf_op jit(solution)/shard_map/ppermute | solution.py:424
  68.3 4.9 %collective-permute-start.21 = (f32[320,128]{1,0:T(8,128)S(1)}, f32[320,128]{1,0:T(8,128)S(1)}, u32[]{:S(2)}, u32[]{:S(2)}) collective-permute-start(f32[320,128]{1,0:T(8,128)S(1)} %add.100), channel_id=1, source_target_pairs={{0,2},{1,3},{2,0},{3,1},{4,6},{5,7},{6,4},{7,5},{8,10},{9,11},{10,... | collective-permute-start | bytes 491528 | tf_op jit(solution)/shard_map/ppermute | solution.py:424
  68.5 8.5 %collective-permute-start.24 = (f32[128,512]{1,0:T(8,128)S(1)}, f32[128,512]{1,0:T(8,128)S(1)}, u32[]{:S(2)}, u32[]{:S(2)}) collective-permute-start(f32[128,512]{1,0:T(8,128)S(1)} %get-tuple-element.38), channel_id=1, source_target_pairs={{0,2},{1,3},{2,4},{3,5},{4,6},{5,7},{6,0},{7,1},{8,10},{9,11},{10,... | collective-permute-start | bytes 786440 | tf_op jit(solution)/shard_map/ppermute | solution.py:405
  70.0 14.8 %collective-permute-start.25 = (f32[128,512]{1,0:T(8,128)S(1)}, f32[128,512]{1,0:T(8,128)S(1)}, u32[]{:S(2)}, u32[]{:S(2)}) collective-permute-start(f32[128,512]{1,0:T(8,128)S(1)} %get-tuple-element.36), channel_id=1, source_target_pairs={{0,4},{1,5},{2,6},{3,7},{4,0},{5,1},{6,2},{7,3},{8,12},{9,13},{10,... | collective-permute-start | bytes 786440 | tf_op jit(solution)/shard_map/ppermute | solution.py:405
  71.1 13.7 %collective-permute-start.26 = (f32[128,512]{1,0:T(8,128)S(1)}, f32[128,512]{1,0:T(8,128)S(1)}, u32[]{:S(2)}, u32[]{:S(2)}) collective-permute-start(f32[128,512]{1,0:T(8,128)S(1)} %get-tuple-element.37), channel_id=1, source_target_pairs={{0,6},{1,7},{2,0},{3,1},{4,2},{5,3},{6,4},{7,5},{8,14},{9,15},{10,... | collective-permute-start | bytes 786440 | tf_op jit(solution)/shard_map/ppermute | solution.py:405
  85.0 6.5 %collective-permute-start.27 = (f32[128,512]{1,0:T(8,128)S(1)}, f32[128,512]{1,0:T(8,128)S(1)}, u32[]{:S(2)}, u32[]{:S(2)}) collective-permute-start(f32[128,512]{1,0:T(8,128)S(1)} %fusion.5), channel_id=1, source_target_pairs={{0,2},{1,3},{2,4},{3,5},{4,6},{5,7},{6,0},{7,1},{8,10},{9,11},{10,... | collective-permute-start | bytes 786440 | tf_op jit(solution)/shard_map/ppermute | solution.py:405
  85.5 13.0 %collective-permute-start.28 = (f32[128,512]{1,0:T(8,128)S(1)}, f32[128,512]{1,0:T(8,128)S(1)}, u32[]{:S(2)}, u32[]{:S(2)}) collective-permute-start(f32[128,512]{1,0:T(8,128)S(1)} %fusion.5), channel_id=1, source_target_pairs={{0,4},{1,5},{2,6},{3,7},{4,0},{5,1},{6,2},{7,3},{8,12},{9,13},{10,... | collective-permute-start | bytes 786440 | tf_op jit(solution)/shard_map/ppermute | solution.py:405
  87.9 11.7 %collective-permute-start.29 = (f32[128,512]{1,0:T(8,128)S(1)}, f32[128,512]{1,0:T(8,128)S(1)}, u32[]{:S(2)}, u32[]{:S(2)}) collective-permute-start(f32[128,512]{1,0:T(8,128)S(1)} %fusion.5), channel_id=1, source_target_pairs={{0,6},{1,7},{2,0},{3,1},{4,2},{5,3},{6,4},{7,5},{8,14},{9,15},{10,... | collective-permute-start | bytes 786440 | tf_op jit(solution)/shard_map/ppermute | solution.py:405
  88.0 13.3 %collective-permute-start.22 = (f32[2,320,128]{2,1,0:T(8,128)S(1)}, f32[2,320,128]{2,1,0:T(8,128)S(1)}, u32[]{:S(2)}, u32[]{:S(2)}) collective-permute-start(f32[2,320,128]{2,1,0:T(8,128)S(1)} %pad_maximum_fusion.1.near), channel_id=1, source_target_pairs={{0,1},{1,0},{2,3},{3,2},{4,5},{5,4},{6,7},{7,6},{8,9},{9,8},{10,11... | collective-permute-start | bytes 983048 | tf_op jit(solution)/shard_map/ppermute | solution.py:404
  99.6 22.3 %collective-permute-start.30 = (f32[4,128,512]{2,1,0:T(8,128)S(1)}, f32[4,128,512]{2,1,0:T(8,128)S(1)}, u32[]{:S(2)}, u32[]{:S(2)}) collective-permute-start(f32[4,128,512]{2,1,0:T(8,128)S(1)} %pad_maximum_fusion.near), channel_id=1, source_target_pairs={{0,1},{1,0},{2,3},{3,2},{4,5},{5,4},{6,7},{7,6},{8,9},{9,8},{10,11... | collective-permute-start | bytes 3145736 | tf_op jit(solution)/shard_map/ppermute | solution.py:404
  111.5 10.5 %copy-start = (bf16[1024,64]{0,1:T(8,128)(2,1)S(1)}, bf16[1024,64]{0,1:T(8,128)(2,1)}, u32[]{:S(2)}) copy-start(bf16[1024,64]{0,1:T(8,128)(2,1)} %param.10) | copy-start | bytes 393220
